TPU v7x, 256 devices: a whole 4x4x8 slice. The times are simulated.
256 devices in a mesh: dp: 16 (over z, core), vocab: 16 (over x, y).
Axes of the slice: x: 4, y: 4, z: 8, core: 2. Of those that a mesh axis runs over, the one named last changes fastest.
Arguments:
- hidden: bfloat16 [4096, 4096], P('dp')
- table: bfloat16 [16384, 4096], P(('vocab', 'dp')), as said below
- targets: int32 [4096], P('dp'), may hold values from 0 to 16383
- token_scale: float32 [4096], P('dp'), may hold values from 2 to 32
- enc_ids: int32 [4096], P(('dp', 'vocab')), may hold values from 0 to 16383
- enc_cot: bfloat16 [4096, 4096], P(('dp', 'vocab')), may hold values from -6 to 6
- dec_ids: int32 [4096], P(('dp', 'vocab')), may hold values from 0 to 16383
- dec_cot: bfloat16 [4096, 4096], P(('dp', 'vocab')), may hold values from -6 to 6
Outputs:
- grad_hidden: bfloat16 [4096, 4096], P('dp', 'vocab')
- grad_table: float32 [16384, 4096], P(('vocab', 'dp'))
- loss: float32 [4096], P('dp')
Inputs may be any that keep to these rules, and one draw needn't show every extreme that they name: table entries of order 3 / sqrt(4096).
All inputs are finite; a program needn't handle non-finite values.
Results may differ from a plain program's by a relative error of at most 0.018.
Values may be sent and summed in bfloat16 or wider, within the bound.
No kernel may reach another device: no remote copies, remote signals or barrier semaphores. Data moves between devices by JAX's collectives and lax.ppermute only.
A program may use at most 128 MiB of HBM per device.

v0:
```python
import jax
import jax.numpy as jnp
from jax import lax
from jax.sharding import PartitionSpec as P


def shards(hidden, table, targets, token_scale, enc_ids, enc_cot, dec_ids, dec_cot):
    vocab_rows = table.shape[0] * lax.axis_size("dp")
    offset = lax.axis_index("vocab") * vocab_rows
    gathered = lax.all_gather(table, "dp", axis=0, tiled=True)
    logits = jnp.dot(hidden, gathered.T, preferred_element_type=jnp.float32)
    local_target = targets - offset
    columns = jnp.arange(vocab_rows, dtype=jnp.int32)
    matches = columns[None, :] == local_target[:, None]
    target_part = jnp.sum(jnp.where(matches, logits, 0.0), axis=1)
    local_max = jnp.max(logits, axis=1)
    row_max = lax.pmax(local_max, "vocab")
    expo = jnp.exp(logits - row_max[:, None])
    row_sum, target_logit = lax.psum((jnp.sum(expo, axis=1), target_part), "vocab")
    loss = row_max + jnp.log(row_sum) - target_logit
    dlogits = (
        token_scale[:, None] * (expo / row_sum[:, None] - matches.astype(jnp.float32))
    ).astype(jnp.bfloat16)
    state_term = jnp.dot(dlogits, gathered, preferred_element_type=jnp.float32)
    grad_hidden = lax.psum_scatter(
        state_term.astype(jnp.bfloat16), "vocab", scatter_dimension=1, tiled=True
    )
    ids_one, cot_one, ids_two, cot_two = (
        lax.all_gather(enc_ids, "vocab", axis=0, tiled=True),
        lax.all_gather(enc_cot, "vocab", axis=0, tiled=True),
        lax.all_gather(dec_ids, "vocab", axis=0, tiled=True),
        lax.all_gather(dec_cot, "vocab", axis=0, tiled=True),
    )
    all_ids = jnp.concatenate([ids_one, ids_two], axis=0) - offset
    all_cot = jnp.concatenate([cot_one, cot_two], axis=0)
    hits = (columns[:, None] == all_ids[None, :]).astype(jnp.bfloat16)
    looked_up = jnp.dot(hits, all_cot, preferred_element_type=jnp.float32)
    head = lax.dot_general(
        dlogits, hidden, (((0,), (0,)), ((), ())), preferred_element_type=jnp.float32
    )
    grad_table = lax.psum_scatter(
        (head + looked_up).astype(jnp.bfloat16), "dp", scatter_dimension=0, tiled=True
    ).astype(jnp.float32)
    return (grad_hidden, grad_table, loss)


def solution(mesh):
    placed = (
        P("dp", None),
        P(("vocab", "dp"), None),
        P("dp"),
        P("dp"),
        P(("dp", "vocab")),
        P(("dp", "vocab"), None),
        P(("dp", "vocab")),
        P(("dp", "vocab"), None),
    )
    return jax.shard_map(
        shards,
        mesh=mesh,
        in_specs=placed,
        out_specs=(P("dp", "vocab"), P(("vocab", "dp"), None), P("dp")),
        check_vma=False,
    )
```

profile of v0, /device:TPU:1, one launch (start us, length us, event | category | flops | bytes accessed | tf_op | source)
XLA Modules:
  0.0 417.5 jit_solution(18154777926044538096)
XLA Ops:
  7.2 0.0 copy-start
  7.2 0.0 all-gather.6.cloned.1.call-start
  7.2 0.7 all-gather.6.cloned.1.call-update
  7.9 0.0 all-gather.8.cloned.1.call-start
  8.0 0.7 all-gather.8.cloned.1.call-update
  8.7 0.0 all-gather.4.cloned.1.call-start
  8.7 0.7 all-gather.4.cloned.1.call-update
  9.4 0.0 reduce-scatter.5.cloned.1.call-start
  9.4 1.3 dynamic-slice
  11.4 0.9 dynamic-update-slice.1
  12.2 0.8 dynamic-update-slice
  13.1 13.8 %all-reduce.2 = (s32[256]{0:T(256)S(1)}, s32[256]{0:T(256)S(1)}) all-reduce(s32[256]{0:T(256)S(1)} %dynamic-update-slice.1, s32[256]{0:T(256)S(1)} %dynamic-update-slice), channel_id=1, replica_groups=mesh['dp'=16,'vocab'=16] {'vocab'}, use_global_device_ids=true, to_apply=%add.1 | all-reduce | flops 512 | bytes 4096
  26.9 0.7 broadcast_subtract_fusion
  27.6 35.8 %all-gather.6.cloned.1.call-done = bf16[256,4096]{1,0:T(8,128)(2,1)} async-done(((bf16[16,4096]{1,0:T(8,128)(2,1)}), bf16[256,4096]{1,0:T(8,128)(2,1)}) %all-gather.6.cloned.1.call-update) | async-done | bytes 2097168 | tf_op jit(solution)/shard_map/all_gather | solution.py:30
  63.4 51.8 %all-gather.8.cloned.1.call-done = bf16[256,4096]{1,0:T(8,128)(2,1)} async-done(((bf16[16,4096]{1,0:T(8,128)(2,1)}), bf16[256,4096]{1,0:T(8,128)(2,1)}) %all-gather.8.cloned.1.call-update) | async-done | bytes 2097168 | tf_op jit(solution)/shard_map/all_gather | solution.py:32
  115.2 10.3 %fusion = f32[1024,4096]{1,0:T(8,128)} fusion(bf16[256,4096]{1,0:T(8,128)(2,1)} %all-gather.8.cloned.1.call-done, bf16[256,4096]{1,0:T(8,128)(2,1)} %all-gather.6.cloned.1.call-done, s32[512]{0:T(512)S(1)} %add_subtract_fusion), kind=kOutput, calls=%fused_computation.2 | convolution fusion | flops 4303880192 | bytes 20973568 | tf_op jit(solution)/shard_map/dot_general | solution.py:37
  125.5 0.0 copy-start.1
  125.5 48.2 %all-gather.4.cloned.1.call-done = bf16[1024,4096]{1,0:T(8,128)(2,1)} async-done(((bf16[64,4096]{1,0:T(8,128)(2,1)}), bf16[1024,4096]{1,0:T(8,128)(2,1)}) %all-gather.4.cloned.1.call-update) | async-done | bytes 8388624 | tf_op jit(solution)/shard_map/all_gather | solution.py:10
  173.7 0.0 copy-done
  173.7 5.8 %fusion.7 = (f32[256]{0:T(256)S(1)}, f32[256,1024]{1,0:T(8,128)S(1)}) fusion(bf16[256,4096]{1,0:T(8,128)(2,1)S(1)} %copy-done, bf16[1024,4096]{1,0:T(8,128)(2,1)} %all-gather.4.cloned.1.call-done), kind=kOutput, calls=%fused_computation.17 | convolution fusion | flops 2147745536 | bytes 11535360 | tf_op jit(solution)/shard_map/dot_general | solution.py:11
  179.5 33.2 %pmax.7 = f32[256]{0:T(256)S(1)} all-reduce(f32[256]{0:T(256)S(1)} %get-tuple-element.9), channel_id=1, replica_groups=mesh['dp'=16,'vocab'=16] {'vocab'}, use_global_device_ids=true, to_apply=%region_1.2 | all-reduce | flops 256 | bytes 2048 | tf_op jit(solution)/shard_map/pmax | solution.py:17
  212.7 0.5 select_reduce_fusion
  213.2 28.8 %all-reduce.3 = (f32[256]{0:T(256)S(1)}, f32[256]{0:T(256)S(1)}) all-reduce(f32[256]{0:T(256)S(1)} %get-tuple-element.4, f32[256]{0:T(256)S(1)} %get-tuple-element.3), channel_id=1, replica_groups=mesh['dp'=16,'vocab'=16] {'vocab'}, use_global_device_ids=true, to_apply=%region_3.4 | all-reduce | flops 512 | bytes 4096 | tf_op jit(solution)/shard_map/psum | solution.py:19
  242.0 0.0 copy-done.1
  242.0 9.2 %add_convert_fusion = bf16[1024,4096]{1,0:T(8,128)(2,1)} fusion(f32[1024,4096]{1,0:T(8,128)} %fusion, bf16[256,4096]{1,0:T(8,128)(2,1)S(1)} %copy-done, f32[256,1024]{1,0:T(8,128)S(1)} %get-tuple-element.10, s32[256]{0:T(256)S(1)} %broadcast_subtract_fusion, f32[256]{0:T(256)S(1)} %get-tuple-element.7, f32[256]{0:T(256)S(1)} %pmax.7, f32[256]{0:T(256)S(1)} %copy-done.1), kind=kOutput, calls=%fused_computation | convolution fusion | flops 2157707264 | bytes 28315648 | tf_op jit(solution)/shard_map/dot_general | solution.py:38
  251.2 0.0 reduce-scatter.5.cloned.1.call-update
  251.2 0.0 reduce-scatter.3.cloned.1.call-start
  251.3 7.4 %convolution_convert_fusion = bf16[256,4096]{1,0:T(8,128)(2,1)} fusion(bf16[1024,4096]{1,0:T(8,128)(2,1)} %all-gather.4.cloned.1.call-done, f32[256,1024]{1,0:T(8,128)S(1)} %get-tuple-element.10, s32[256]{0:T(256)S(1)} %broadcast_subtract_fusion, f32[256]{0:T(256)S(1)} %get-tuple-element.7, f32[256]{0:T(256)S(1)} %pmax.7, f32[256]{0:T(256)S(1)} %copy-done.1), kind=kOutput, calls=%fused_computation.1 | convolution fusion | flops 2150367232 | bytes 11538432 | tf_op jit(solution)/shard_map/dot_general | solution.py:24
  258.6 0.0 reduce-scatter.3.cloned.1.call-update
  258.7 0.6 add_subtract_fusion.1
  259.2 68.2 %reduce-scatter.5.cloned.1.call-done = bf16[64,4096]{1,0:T(8,128)(2,1)} async-done(((bf16[1024,4096]{1,0:T(8,128)(2,1)}), bf16[64,4096]{1,0:T(8,128)(2,1)}) %reduce-scatter.5.cloned.1.call-update) | async-done | bytes 524304 | tf_op jit(solution)/shard_map/reduce_scatter | solution.py:41
  327.4 2.1 convert_element_type.20
  329.5 81.4 %reduce-scatter.3.cloned.1.call-done = bf16[256,256]{1,0:T(8,128)(2,1)} async-done(((bf16[256,4096]{1,0:T(8,128)(2,1)}), bf16[256,256]{1,0:T(8,128)(2,1)}) %reduce-scatter.3.cloned.1.call-update) | async-done | bytes 131088 | tf_op jit(solution)/shard_map/reduce_scatter | solution.py:25
  (3 shorter events, 0.0 us)
Async XLA Ops:
  7.2 166.5 %copy-start = (bf16[256,4096]{1,0:T(8,128)(2,1)S(1)}, bf16[256,4096]{1,0:T(8,128)(2,1)}, u32[]{:S(2)}) copy-start(bf16[256,4096]{1,0:T(8,128)(2,1)} %param.8) | copy-start | bytes 6291460
  7.2 56.2 %all-gather.6.cloned.1.call-start = ((), (), s32[]{:S(2)}) async-start(), calls=%async_computation.4 | async-start | bytes 2228224 | tf_op jit(solution)/shard_map/all_gather | solution.py:30
  7.9 107.3 %all-gather.8.cloned.1.call-start = ((), (), s32[]{:S(2)}) async-start(), calls=%async_computation.5 | async-start | bytes 2228224 | tf_op jit(solution)/shard_map/all_gather | solution.py:32
  8.7 165.0 %all-gather.4.cloned.1.call-start = ((), (), s32[]{:S(2)}) async-start(), calls=%async_computation.2 | async-start | bytes 8912896 | tf_op jit(solution)/shard_map/all_gather | solution.py:10
  9.4 318.1 %reduce-scatter.5.cloned.1.call-start = ((), (), s32[]{:S(2)}) async-start(), calls=%async_computation.6 | async-start | bytes 8912896 | tf_op jit(solution)/shard_map/reduce_scatter | solution.py:41
  125.5 116.5 %copy-start.1 = (f32[256]{0:T(256)S(1)}, f32[256]{0:T(256)}, u32[]{:S(2)}) copy-start(f32[256]{0:T(256)} %param.11) | copy-start | bytes 3076
  251.2 159.7 %reduce-scatter.3.cloned.1.call-start = ((), (), s32[]{:S(2)}) async-start(), calls=%async_computation.3 | async-start | bytes 2228224 | tf_op jit(solution)/shard_map/reduce_scatter | solution.py:25
Sparse Core Ops, SparseCore 0:
  10.4 52.8 all-gather.5
  65.8 49.3 all-gather.7
  117.0 56.5 all-gather.3
  251.3 76.0 reduce-scatter.4
  331.4 79.4 reduce-scatter.2
where the time goes:
time: 418 us; the launch traced here: 417 us
  waiting for transfers between devices  287 us (69%)
  blocking collectives  75.8 us (18%)
  matrix products  32.7 us (8%)
  between operations  14.5 us (3%)
    reduce_scatter x1, waiting for transfers between devices, shards(): lax.psum_scatter(state_term.astype(jnp.bfloat16), 'vocab', scatter_dimens...  81.4 us
    reduce_scatter x1, waiting for transfers between devices, shards(): lax.psum_scatter((head + looked_up).astype(jnp.bfloat16), 'dp', scatter_d...  68.2 us
    all_gather x1, waiting for transfers between devices, shards(): lax.all_gather(dec_cot, 'vocab', axis=0, tiled=True)  51.8 us
    all_gather x1, waiting for transfers between devices, shards(): gathered = lax.all_gather(table, 'dp', axis=0, tiled=True)  48.2 us
    all_gather x1, waiting for transfers between devices, shards(): lax.all_gather(enc_cot, 'vocab', axis=0, tiled=True)  35.8 us
    pmax x1, blocking collectives, shards(): row_max = lax.pmax(local_max, 'vocab')  33.2 us
    psum x1, blocking collectives, shards(): lax.psum((jnp.sum(expo, axis=1), target_part), 'vocab')  28.8 us
    unnamed x1, blocking collectives  13.8 us
  transfers between devices with their start and end apart: 5, of which 5 were waited for; matrix products, arithmetic and copies ran while one was open for 6% of the time, Pallas kernels for 0%

commit v1 on v0

v1 whole, which is shorter than its diff:
```python
import jax
import jax.numpy as jnp
from jax import lax
from jax.experimental import pallas as pl
from jax.experimental.pallas import tpu as pltpu
from jax.sharding import Mesh, PartitionSpec as P

bf16, f32, i32 = jnp.bfloat16, jnp.float32, jnp.int32
NX, NY, NZ = 4, 4, 8
PARAMS = pltpu.CompilerParams(vmem_limit_bytes=40 << 20)
ALONE = pltpu.CompilerParams(vmem_limit_bytes=60 << 20)


def shift(x, k):
    return lax.ppermute(x, "z", [(i, (i + k) % NZ) for i in range(NZ)])


def swap(x):
    return lax.ppermute(x, "c", [(0, 1), (1, 0)])


def after(x, *others):
    return lax.optimization_barrier((x,) + others)[0]


def legs(leg):
    groups = []
    for c in range(2):
        for i in range(4):
            places = [(j, i) if c == leg else (i, j) for j in range(4)]
            groups.append([(c * NX + x) * NY + y for x, y in places])
    return groups


def exchange(x, leg):
    return lax.all_to_all(
        x, ("c", "x", "y"), 0, 0, axis_index_groups=legs(leg), tiled=True
    )


def cost(flops, moved):
    return pl.CostEstimate(flops=flops, bytes_accessed=moved, transcendentals=0)


def stats_body(logits_ref, names_ref, wanted_ref, out_ref):
    logits = logits_ref[...]
    top = jnp.max(logits, axis=0, keepdims=True)
    out_ref[0:1] = top
    out_ref[1:2] = jnp.sum(jnp.exp(logits - top), axis=0, keepdims=True)
    hit = names_ref[...] == wanted_ref[...]
    out_ref[2:3] = jnp.sum(jnp.where(hit, logits, 0.0), axis=0, keepdims=True)


def head_body(
    starts, logits_ref, names_ref, tokens_ref, wanted_ref, in_order_ref, ids_ref,
    own_ref, other_ref, cots_ref, out_ref, d_ref, sorted_ref, hits_ref,
):
    @pl.when(pl.program_id(0) == 0)
    def _():
        rows = d_ref.shape[0] // NZ
        share = jnp.exp(logits_ref[...] - tokens_ref[0:1]) / tokens_ref[1:2]
        hit = (names_ref[...] == wanted_ref[...]).astype(f32)
        d_ref[...] = (tokens_ref[2:3] * (share - hit)).astype(bf16)
        for k in range(NZ):
            start = pl.multiple_of(starts[k], rows)
            sorted_ref[pl.ds(start, rows), :] = d_ref[k * rows : (k + 1) * rows]
        hits_ref[...] = (in_order_ref[...] == ids_ref[...]).astype(f32).astype(bf16)

    tokens = own_ref.shape[0]
    term = jnp.dot(hits_ref[...], cots_ref[...], preferred_element_type=f32)
    term += jnp.dot(sorted_ref[:, :tokens], own_ref[...], preferred_element_type=f32)
    term += jnp.dot(sorted_ref[:, tokens:], other_ref[...], preferred_element_type=f32)
    out_ref[...] = term.astype(bf16)


def state_body(order, d_ref, *refs):
    *table_refs, own_ref, their_ref, turned = refs

    @pl.when(pl.program_id(0) == 0)
    def _():
        turned[...] = d_ref[...].astype(f32).T.astype(bf16)

    start, term = 0, 0.0
    for t_ref in table_refs:
        stop = start + t_ref.shape[0]
        term += jnp.dot(turned[:, start:stop], t_ref[...], preferred_element_type=f32)
        start = stop
    tokens = own_ref.shape[1]
    own_ref[0] = term[:tokens].astype(bf16)
    their_ref[0] = term[tokens:].astype(bf16)


def shards(hidden, table, targets, token_scale, enc_ids, enc_cot, dec_ids, dec_cot):
    rows, depth = table.shape
    tokens = hidden.shape[0]
    vocab = rows * NZ
    z, c = lax.axis_index("z"), lax.axis_index("c")
    x, y = lax.axis_index("x"), lax.axis_index("y")
    base = (x * NY + y) * (vocab * 2)

    ids = jnp.concatenate([enc_ids, dec_ids])
    lane = lax.broadcasted_iota(i32, (ids.shape[0], 128), 1)
    tail = jnp.where(
        lane == 0, (ids // 128)[:, None], jnp.where(lane == 1, (ids % 128)[:, None], 0)
    ).astype(bf16)
    cots = jnp.concatenate([jnp.concatenate([enc_cot, dec_cot], 0), tail], 1)
    cots = lax.all_gather(cots, ("c", "x", "y"), axis=0, tiled=True)
    ids = cots[:, depth : depth + 2].astype(i32)
    ids = (ids[:, 0] * 128 + ids[:, 1])[None]
    n_ids = ids.shape[1]
    peers = 2 * NX * NY

    half = rows // 2
    up, down = shift(table, 1), shift(table, -1)
    blocks = {0: table, -1: up, 1: down}
    other, wanted, scales = swap(hidden), swap(targets), swap(token_scale)
    wanted = jnp.concatenate([targets, wanted])[None]
    scales = jnp.concatenate([token_scale, scales])[None]
    for k in range(2, NZ // 2):
        up, down = lax.optimization_barrier((up, down, other, wanted, scales))[:2]
        up, down = shift(up, 1), shift(down, -1)
        blocks[-k], blocks[k] = up, down
    up, down = shift(up[:half], 1), shift(down[half:], -1)
    blocks[NZ // 2] = jnp.concatenate([up, down], 0)

    order = [[0, 1, -1, 2], [-2, 3, -3], [NZ // 2]]
    parts = [jnp.concatenate([blocks[k] for k in g], 0) for g in order]
    parts = [lax.optimization_barrier(part) for part in parts]
    states = jnp.concatenate([hidden, other], 0)
    logits = jnp.concatenate(
        [
            lax.dot_general(g, states, (((1,), (1,)), ((), ())), preferred_element_type=f32)
            for g in parts
        ],
        0,
    )
    places = jnp.array([k for g in order for k in g], i32)
    places = (z + places + NZ) % NZ
    spread = jnp.arange(rows, dtype=i32)
    names = ((base + (places * 2 + c) * rows)[:, None] + spread).reshape(vocab, 1)
    in_order = ((base + (jnp.arange(NZ, dtype=i32) * 2 + c) * rows)[:, None] + spread).reshape(vocab, 1)

    stats = pl.pallas_call(
        stats_body,
        out_shape=jax.ShapeDtypeStruct((3, 2 * tokens), f32),
        compiler_params=PARAMS,
        cost_estimate=cost(8 * vocab * tokens, 8 * vocab * tokens),
        name="stats",
    )(logits, names, wanted)
    turned = jnp.concatenate([stats[:, tokens:], stats[:, :tokens]], 1)
    stats = jnp.where(jnp.arange(2)[:, None, None] == c, stats[None], turned[None])
    stats = jnp.broadcast_to(stats[:, None], (2, NX * NY) + stats.shape[1:])
    stats = lax.all_to_all(
        stats.reshape((peers,) + stats.shape[2:]), ("c", "x", "y"), 0, 0, tiled=True
    )

    row_max = jnp.max(stats[:, 0], axis=0)
    row_sum = jnp.sum(stats[:, 1] * jnp.exp(stats[:, 0] - row_max), axis=0)
    loss = row_max + jnp.log(row_sum) - jnp.sum(stats[:, 2], axis=0)

    width = 512
    head, dlogits = pl.pallas_call(
        head_body,
        out_shape=(
            jax.ShapeDtypeStruct((vocab, depth), bf16),
            jax.ShapeDtypeStruct((vocab, 2 * tokens), bf16),
        ),
        grid_spec=pltpu.PrefetchScalarGridSpec(
            num_scalar_prefetch=1,
            grid=(depth // width,),
            in_specs=[
                pl.BlockSpec((vocab, 2 * tokens), lambda i, s: (0, 0)),
                pl.BlockSpec((vocab, 1), lambda i, s: (0, 0)),
                pl.BlockSpec((3, 2 * tokens), lambda i, s: (0, 0)),
                pl.BlockSpec((1, 2 * tokens), lambda i, s: (0, 0)),
                pl.BlockSpec((vocab, 1), lambda i, s: (0, 0)),
                pl.BlockSpec((1, n_ids), lambda i, s: (0, 0)),
                pl.BlockSpec((tokens, width), lambda i, s: (0, i)),
                pl.BlockSpec((tokens, width), lambda i, s: (0, i)),
                pl.BlockSpec((n_ids, width), lambda i, s: (0, i)),
            ],
            out_specs=(
                pl.BlockSpec((vocab, width), lambda i, s: (0, i)),
                pl.BlockSpec((vocab, 2 * tokens), lambda i, s: (0, 0)),
            ),
            scratch_shapes=[
                pltpu.VMEM((vocab, 2 * tokens), bf16),
                pltpu.VMEM((vocab, n_ids), bf16),
            ],
        ),
        compiler_params=ALONE,
        cost_estimate=cost(
            2 * vocab * (2 * tokens + n_ids) * depth, 2 * (vocab + 2 * tokens + n_ids) * depth
        ),
        name="head",
    )(
        places * rows, logits, names, jnp.concatenate([row_max[None], row_sum[None], scales]),
        wanted, in_order, ids, hidden, other, cots,
    )
    grad_table = lax.psum_scatter(head, "z", scatter_dimension=0, tiled=True).astype(f32)

    width = depth // (NX * NY)
    spot = jnp.arange(NX * NY, dtype=i32)
    spot = jnp.where(c == 0, spot, spot % 4 * 4 + spot // 4)
    out = pl.BlockSpec((1, tokens, width), lambda i, order: (i // 4, 0, i % 4))
    given = pl.BlockSpec((1, tokens, width), lambda i, order: (i % 4, 0, i // 4))
    own, theirs = pl.pallas_call(
        state_body,
        out_shape=(jax.ShapeDtypeStruct((4, tokens, depth // 4), bf16),) * 2,
        grid_spec=pltpu.PrefetchScalarGridSpec(
            num_scalar_prefetch=1,
            grid=(NX * NY,),
            in_specs=[
                pl.BlockSpec((vocab, 2 * tokens), lambda i, order: (0, 0)),
            ]
            + [pl.BlockSpec((p.shape[0], width), lambda i, order: (0, order[i])) for p in parts],
            out_specs=(out, given),
            scratch_shapes=[pltpu.VMEM((2 * tokens, vocab), bf16)],
        ),
        compiler_params=PARAMS,
        cost_estimate=cost(4 * vocab * tokens * depth, 2 * (vocab + 2 * tokens) * depth),
        name="state_terms",
    )(spot, dlogits, *parts)
    term = (own.astype(f32) + swap(theirs).astype(f32)).astype(bf16)
    term = jnp.sum(exchange(term, 0).astype(f32), 0)
    term = jnp.stack([term[:, i * width : (i + 1) * width] for i in range(4)]).astype(bf16)
    grad_hidden = jnp.sum(exchange(term, 1).astype(f32), 0).astype(bf16)
    return (grad_hidden, grad_table, loss[:tokens])


def solution(mesh):
    fine = Mesh(mesh.devices.reshape(NZ, 2, NX, NY), ("z", "c", "x", "y"))
    dp, vocab, every = ("z", "c"), ("x", "y"), ("z", "c", "x", "y")
    return jax.shard_map(
        shards,
        mesh=fine,
        in_specs=(
            P(dp, None), P(vocab + dp, None), P(dp), P(dp),
            P(every), P(every, None), P(every), P(every, None),
        ),
        out_specs=(P(dp, vocab), P(vocab + dp, None), P(dp)),
        check_vma=False,
    )
```

time: 418 us -> 166 us (0.40)
  waiting for transfers between devices: 287 us -> 53.2 us
  blocking collectives: 75.8 us -> 18.1 us
  matrix products: 32.7 us -> 4.2 us
  starting transfers between devices: 0.19 us -> 27.4 us
  Pallas kernels: 0 us -> 22.8 us
  other arithmetic: 3.81 us -> 13.7 us
  local copies, waits for them, and re-layouts: 2.98 us -> 11.6 us
    reduce_scatter x2 -> x1, waiting for transfers between devices: 150 us -> 2.2 us  [shards(): lax.psum_scatter(head, 'z', scatter_dimension=0, tiled=True).astype(f32)]
    all_gather x3 -> x1, waiting for transfers between devices: 136 us -> 0.01 us  [shards(): cots = lax.all_gather(cots, ('c', 'x', 'y'), axis=0, tiled=True)]
    ppermute x0 -> x12, waiting for transfers between devices: none -> 36.4 us  [the longest x8 32.6 us: shift(): return lax.ppermute(x, 'z', [(i, (i + k) % NZ) for i in range(NZ)])]
    pmax x1 -> x0, blocking collectives: 33.2 us -> none  [shards(): row_max = lax.pmax(local_max, 'vocab')]
    psum x1 -> x0, blocking collectives: 28.8 us -> none  [shards(): lax.psum((jnp.sum(expo, axis=1), target_part), 'vocab')]
    dot_general x4 -> x3, matrix products: 32.7 us -> 4.2 us  [shards(): lax.dot_general(g, states, (((1,), (1,)), ((), ())), preferred_element_ty...]
    pallas_call x0 -> x3, Pallas kernels: none -> 22.8 us  [the longest x1 13.9 us: shards(): pl.pallas_call(head_body, out_shape=(jax.ShapeDtypeStruct((vocab, depth),...]
    all_to_all x0 -> x1, blocking collectives: none -> 18.1 us  [exchange(): lax.all_to_all(x, ('c', 'x', 'y'), 0, 0, axis_index_groups=legs(leg), til...]
  transfers between devices with their start and end apart: 5 -> 16, of which waited for: 5 -> 12; matrix products, arithmetic and copies ran while one was open for 6% -> 11% of each run, Pallas kernels for 0% -> 5%
where the time goes in v1:
time: 166 us; the launch traced here: 165 us
  waiting for transfers between devices  53.2 us (32%)
  starting transfers between devices  27.4 us (17%)
  Pallas kernels  22.8 us (14%)
  blocking collectives  18.1 us (11%)
  between operations  14.3 us (9%)
  other arithmetic  13.7 us (8%)
  local copies, waits for them, and re-layouts  11.6 us (7%)
  matrix products  4.2 us (3%)
    ppermute x8, waiting for transfers between devices, shift(): return lax.ppermute(x, 'z', [(i, (i + k) % NZ) for i in range(NZ)])  32.6 us
    all_to_all x1, blocking collectives, exchange(): lax.all_to_all(x, ('c', 'x', 'y'), 0, 0, axis_index_groups=legs(leg), til...  18.1 us
    pallas_call x1, Pallas kernels, shards(): pl.pallas_call(head_body, out_shape=(jax.ShapeDtypeStruct((vocab, depth),...  13.9 us
    all_to_all x1, starting transfers between devices, shards(): lax.all_to_all(stats.reshape((peers,) + stats.shape[2:]), ('c', 'x', 'y')...  10.7 us
    ppermute x8, starting transfers between devices, shift(): return lax.ppermute(x, 'z', [(i, (i + k) % NZ) for i in range(NZ)])  8.59 us
    pallas_call x1, Pallas kernels, shards(): pl.pallas_call(state_body, out_shape=(jax.ShapeDtypeStruct((4, tokens, de...  8.51 us
    all_to_all x1, waiting for transfers between devices, shards(): lax.all_to_all(stats.reshape((peers,) + stats.shape[2:]), ('c', 'x', 'y')...  8.26 us
    unnamed x31, local copies, waits for them, and re-layouts  7.59 us
  transfers between devices with their start and end apart: 16, of which 12 were waited for; matrix products, arithmetic and copies ran while one was open for 11% of the time, Pallas kernels for 5%

profile of v1, /device:TPU:1, one launch (start us, length us, event | category | flops | bytes accessed | tf_op | source)
XLA Modules:
  0.0 165.4 jit_solution(3596167883029211941)
XLA Ops:
  7.2 0.8 and_select_fusion.1
  8.0 0.1 select_convert_fusion
  8.1 1.7 %pad_maximum_fusion.5 = bf16[32,4224]{1,0:T(8,128)(2,1)} fusion(bf16[32,128]{1,0:T(8,128)(2,1)S(1)} %select_convert_fusion, bf16[16,4096]{1,0:T(8,128)(2,1)} %param.16, bf16[16,4096]{1,0:T(8,128)(2,1)} %param.14), kind=kLoop, calls=%fused_computation.9 | loop fusion | flops 811008 | bytes 540672 | tf_op jit(solution)/shard_map/concatenate | solution.py:106
  9.8 3.3 %collective-permute-start.2 = (bf16[256,4096]{1,0:T(8,128)(2,1)}, bf16[256,4096]{1,0:T(8,128)(2,1)S(1)}, u32[]{:S(2)}, u32[]{:S(2)}) collective-permute-start(bf16[256,4096]{1,0:T(8,128)(2,1)} %own_ref.1), channel_id=1, source_target_pairs={{0,16},{16,0},{1,17},{17,1},{2,18},{18,2},{3,19},{19,3},{4,20},{20... | collective-permute-start | bytes 6291464 | tf_op jit(solution)/shard_map/ppermute | solution.py:19
  13.2 3.9 %collective-permute-start = (bf16[64,4096]{1,0:T(8,128)(2,1)}, bf16[64,4096]{1,0:T(8,128)(2,1)S(1)}, u32[]{:S(2)}, u32[]{:S(2)}) collective-permute-start(bf16[64,4096]{1,0:T(8,128)(2,1)} %param.10), channel_id=1, source_target_pairs={{0,224},{32,0},{64,32},{96,64},{128,96},{160,128},{192,160},{224,1... | collective-permute-start | bytes 1572872 | tf_op jit(solution)/shard_map/ppermute | solution.py:15
  17.0 0.4 collective-permute-start.3
  17.4 0.2 collective-permute-start.4
  17.5 0.7 multiply_add_fusion.1
  18.2 3.2 %constant_dynamic-update-slice_fusion.1 = bf16[512,4096]{1,0:T(8,128)(2,1)} fusion(bf16[256,4096]{1,0:T(8,128)(2,1)} %own_ref.1), kind=kLoop, calls=%fused_computation.26 | loop fusion | bytes 4194304
  21.4 0.1 iota_add_fusion.1
  21.5 0.1 iota_add_fusion
  21.6 7.0 %collective-permute-done = bf16[64,4096]{1,0:T(8,128)(2,1)S(1)} collective-permute-done((bf16[64,4096]{1,0:T(8,128)(2,1)}, bf16[64,4096]{1,0:T(8,128)(2,1)S(1)}, u32[]{:S(2)}, u32[]{:S(2)}) %collective-permute-start) | collective-permute-done | bytes 524320 | tf_op jit(solution)/shard_map/ppermute | solution.py:15
  28.6 3.1 %collective-permute-done.1 = bf16[64,4096]{1,0:T(8,128)(2,1)S(1)} collective-permute-done((bf16[64,4096]{1,0:T(8,128)(2,1)}, bf16[64,4096]{1,0:T(8,128)(2,1)S(1)}, u32[]{:S(2)}, u32[]{:S(2)}) %collective-permute-start.1) | collective-permute-done | bytes 524320 | tf_op jit(solution)/shard_map/ppermute | solution.py:15
  31.7 0.8 copy-done.11
  32.5 0.2 collective-permute-start.5
  32.7 1.2 collective-permute-start.6
  34.0 0.2 add.165.names_ref
  34.2 0.9 add.164.in_order_ref
  35.1 1.5 constant_dynamic-update-slice_fusion
  36.6 8.4 %collective-permute-done.5 = bf16[64,4096]{1,0:T(8,128)(2,1)} collective-permute-done((bf16[64,4096]{1,0:T(8,128)(2,1)S(1)}, bf16[64,4096]{1,0:T(8,128)(2,1)}, u32[]{:S(2)}, u32[]{:S(2)}) %collective-permute-start.5) | collective-permute-done | bytes 524320 | tf_op jit(solution)/shard_map/ppermute | solution.py:15
  44.9 1.5 collective-permute-done.6
  46.4 0.8 copy-done.8
  47.2 0.2 collective-permute-start.7
  47.4 1.3 collective-permute-start.8
  48.7 1.6 pad_maximum_fusion.refs_0_
  50.3 1.3 fusion.9
  51.6 0.1 copy-done.1
  51.7 7.2 %collective-permute-done.7 = bf16[64,4096]{1,0:T(8,128)(2,1)S(1)} collective-permute-done((bf16[64,4096]{1,0:T(8,128)(2,1)}, bf16[64,4096]{1,0:T(8,128)(2,1)S(1)}, u32[]{:S(2)}, u32[]{:S(2)}) %collective-permute-start.7) | collective-permute-done | bytes 524320 | tf_op jit(solution)/shard_map/ppermute | solution.py:15
  58.9 1.4 collective-permute-done.8
  60.3 0.1 pad_maximum_fusion.1.refs_1_
  60.5 0.4 collective-permute-start.10
  60.9 1.4 collective-permute-start.9
  62.3 1.5 fusion.10
  63.9 2.3 %collective-permute-done.10 = bf16[32,4096]{1,0:T(8,128)(2,1)S(1)} collective-permute-done((bf16[32,4096]{1,0:T(8,128)(2,1)S(1)}, bf16[32,4096]{1,0:T(8,128)(2,1)S(1)}, u32[]{:S(2)}, u32[]{:S(2)}) %collective-permute-start.10) | collective-permute-done | bytes 262176 | tf_op jit(solution)/shard_map/ppermute | solution.py:15
  66.2 1.8 %collective-permute-done.9 = bf16[32,4096]{1,0:T(8,128)(2,1)S(1)} collective-permute-done((bf16[32,4096]{1,0:T(8,128)(2,1)S(1)}, bf16[32,4096]{1,0:T(8,128)(2,1)S(1)}, u32[]{:S(2)}, u32[]{:S(2)}) %collective-permute-start.9) | collective-permute-done | bytes 262176 | tf_op jit(solution)/shard_map/ppermute | solution.py:15
  68.0 1.4 fusion.11
  69.4 0.1 pad_maximum_fusion.2.logits_ref
  69.5 0.4 stats.1
  69.9 0.1 broadcast_select_fusion
  70.0 0.8 broadcast_in_dim.76
  70.8 10.7 %all-to-all-start = ((f32[32,3,512]{2,1,0:T(4,128)}), f32[32,3,512]{2,1,0:T(4,128)S(1)}, u32[]{:S(2)}, u32[]{:S(2)}) async-start(f32[32,3,512]{2,1,0:T(4,128)} %bitcast.2), calls=%async_computation | async-start | bytes 524288 | tf_op jit(solution)/shard_map/all_to_all | solution.py:153
  81.5 0.0 reduce-scatter.2.cloned.1.call-start
  81.5 0.5 broadcast_multiply_fusion.starts
  82.0 8.3 %all-to-all-done = f32[32,3,512]{2,1,0:T(4,128)S(1)} async-done(((f32[32,3,512]{2,1,0:T(4,128)}), f32[32,3,512]{2,1,0:T(4,128)S(1)}, u32[]{:S(2)}, u32[]{:S(2)}) %all-to-all-start) | async-done | bytes 196640 | tf_op jit(solution)/shard_map/all_to_all | solution.py:153
  90.3 0.2 slice_reduce_fusion
  90.5 0.6 pad_maximum_fusion.7.tokens_ref
  91.1 1.0 slice_convert_fusion
  92.1 1.0 fusion
  93.1 13.9 %head.1 = (bf16[512,4096]{1,0:T(8,128)(2,1)}, bf16[512,512]{1,0:T(8,128)(2,1)}) custom-call(s32[8]{0:T(128)} %broadcast_multiply_fusion.starts, f32[512,512]{1,0:T(8,128)} %copy-done, s32[512,1]{1,0:T(8,128)} %copy-done.3, f32[3,512]{1,0:T(4,128)} %pad_maximum_fusion.7.tokens_ref, s32[1,512]{1,0:T(1,128)} %bitcast.33, s32[512,1]{1,0:T(8,128)} %add.164.in_order_ref, ...), custom_call_target="tpu_custom_call" | custom-call | flops 6442450944 | bytes 16777216 | tf_op jit(solution)/shard_map/head/pallas_call | solution.py:162
  107.1 1.0 copy-done.5
  108.1 1.6 copy-done.2
  109.6 8.5 %state_terms.1 = (bf16[4,256,1024]{2,1,0:T(8,128)(2,1)S(1)}, bf16[4,256,1024]{2,1,0:T(8,128)(2,1)S(1)}) custom-call(s32[16]{0:T(128)S(1)} %broadcast_select_fusion.1.order, bf16[512,512]{1,0:T(8,128)(2,1)S(1)} %copy-done.5, bf16[256,4096]{1,0:T(8,128)(2,1)S(1)} %copy-done.2, bf16[192,4096]{1,0:T(8,128)(2,1)S(1)} %pad_maximum_fusion.1.refs_1_, ...), custom_call_target="tpu_custom_call" | custom-call | flops 2147483648 | bytes 8388608 | tf_op jit(solution)/shard_map/state_terms/pallas_call | solution.py:207
  118.2 0.7 collective-permute-start.11
  118.9 3.8 %collective-permute-done.11 = bf16[4,256,1024]{2,1,0:T(8,128)(2,1)S(1)} collective-permute-done((bf16[4,256,1024]{2,1,0:T(8,128)(2,1)S(1)}, bf16[4,256,1024]{2,1,0:T(8,128)(2,1)S(1)}, u32[]{:S(2)}, u32[]{:S(2)}) %collective-permute-start.11) | collective-permute-done | bytes 2097184 | tf_op jit(solution)/shard_map/ppermute | solution.py:19
  122.7 1.0 add_convert_fusion
  123.7 18.1 %all_to_all.15 = bf16[4,256,1024]{2,1,0:T(8,128)(2,1)S(1)} all-to-all(bf16[4,256,1024]{2,1,0:T(8,128)(2,1)S(1)} %add_convert_fusion), channel_id=1, replica_groups={{0,4,8,12},{1,5,9,13},{2,6,10,14},{3,7,11,15},{16,17,18,19},{20,21,22,2..., dimensions={0} | all-to-all | bytes 4194304 | tf_op jit(solution)/shard_map/all_to_all | solution.py:36
  141.8 0.4 reduce.3
  142.3 0.9 pad_maximum_fusion.4
  143.1 3.5 %all-to-all-start.2 = ((bf16[4,256,256]{2,1,0:T(8,128)(2,1)}), bf16[4,256,256]{2,1,0:T(8,128)(2,1)S(1)}, u32[]{:S(2)}, u32[]{:S(2)}) async-start(bf16[4,256,256]{2,1,0:T(8,128)(2,1)} %pad_maximum_fusion.4), calls=%async_computation.2 | async-start | bytes 1048576 | tf_op jit(solution)/shard_map/all_to_all | solution.py:36
  146.6 0.6 slice.64
  147.2 6.3 %all-to-all-done.2 = bf16[4,256,256]{2,1,0:T(8,128)(2,1)S(1)} async-done(((bf16[4,256,256]{2,1,0:T(8,128)(2,1)}), bf16[4,256,256]{2,1,0:T(8,128)(2,1)S(1)}, u32[]{:S(2)}, u32[]{:S(2)}) %all-to-all-start.2) | async-done | bytes 524320 | tf_op jit(solution)/shard_map/all_to_all | solution.py:36
  153.5 0.7 reduce_sum.41
  154.2 2.2 %reduce-scatter.2.cloned.1.call-done = bf16[64,4096]{1,0:T(8,128)(2,1)} async-done(((bf16[512,4096]{1,0:T(8,128)(2,1)}), bf16[64,4096]{1,0:T(8,128)(2,1)}) %reduce-scatter.2.cloned.1.call-update) | async-done | bytes 524304 | tf_op jit(solution)/shard_map/reduce_scatter | solution.py:200
  156.4 2.1 %convert_element_type.30 = f32[64,4096]{1,0:T(8,128)} convert(bf16[64,4096]{1,0:T(8,128)(2,1)} %reduce-scatter.2.cloned.1.call-done) | non-fusion elementwise | flops 262144 | bytes 1572864 | tf_op jit(solution)/shard_map/convert_element_type | solution.py:200
  (47 shorter events, 0.3 us)
Async XLA Ops:
  7.2 14.4 %copy-start.13 = (s32[256]{0:T(256)S(1)}, s32[256]{0:T(256)}, u32[]{:S(2)}) copy-start(s32[256]{0:T(256)} %param.11) | copy-start | bytes 3076
  7.2 14.4 %copy-start.14 = (f32[256]{0:T(256)S(1)}, f32[256]{0:T(256)}, u32[]{:S(2)}) copy-start(f32[256]{0:T(256)} %param.12) | copy-start | bytes 3076
  7.2 83.9 %all-gather.2.cloned.1.call-start = ((), (), s32[]{:S(2)}) async-start(), calls=%async_computation.4 | async-start | bytes 8921088 | tf_op jit(solution)/shard_map/all_gather | solution.py:107
  9.8 21.9 %collective-permute-start.2 = (bf16[256,4096]{1,0:T(8,128)(2,1)}, bf16[256,4096]{1,0:T(8,128)(2,1)S(1)}, u32[]{:S(2)}, u32[]{:S(2)}) collective-permute-start(bf16[256,4096]{1,0:T(8,128)(2,1)} %own_ref.1), channel_id=1, source_target_pairs={{0,16},{16,0},{1,17},{17,1},{2,18},{18,2},{3,19},{19,3},{4,20},{20... | collective-permute-start | bytes 6291464 | tf_op jit(solution)/shard_map/ppermute | solution.py:19
  13.2 15.4 %collective-permute-start = (bf16[64,4096]{1,0:T(8,128)(2,1)}, bf16[64,4096]{1,0:T(8,128)(2,1)S(1)}, u32[]{:S(2)}, u32[]{:S(2)}) collective-permute-start(bf16[64,4096]{1,0:T(8,128)(2,1)} %param.10), channel_id=1, source_target_pairs={{0,224},{32,0},{64,32},{96,64},{128,96},{160,128},{192,160},{224,1... | collective-permute-start | bytes 1572872 | tf_op jit(solution)/shard_map/ppermute | solution.py:15
  17.0 14.7 %collective-permute-start.1 = (bf16[64,4096]{1,0:T(8,128)(2,1)}, bf16[64,4096]{1,0:T(8,128)(2,1)S(1)}, u32[]{:S(2)}, u32[]{:S(2)}) collective-permute-start(bf16[64,4096]{1,0:T(8,128)(2,1)} %param.10), channel_id=1, source_target_pairs={{0,32},{32,64},{64,96},{96,128},{128,160},{160,192},{192,224},{224... | collective-permute-start | bytes 1572872 | tf_op jit(solution)/shard_map/ppermute | solution.py:15
  17.0 4.6 %collective-permute-start.3 = (s32[256]{0:T(256)}, s32[256]{0:T(256)S(1)}, u32[]{:S(2)}, u32[]{:S(2)}) collective-permute-start(s32[256]{0:T(256)} %param.11), channel_id=1, source_target_pairs={{0,16},{16,0},{1,17},{17,1},{2,18},{18,2},{3,19},{19,3},{4,20},{20... | collective-permute-start | bytes 3080 | tf_op jit(solution)/shard_map/ppermute | solution.py:19
  17.4 4.2 %collective-permute-start.4 = (f32[256]{0:T(256)}, f32[256]{0:T(256)S(1)}, u32[]{:S(2)}, u32[]{:S(2)}) collective-permute-start(f32[256]{0:T(256)} %param.12), channel_id=1, source_target_pairs={{0,16},{16,0},{1,17},{17,1},{2,18},{18,2},{3,19},{19,3},{4,20},{20... | collective-permute-start | bytes 3080 | tf_op jit(solution)/shard_map/ppermute | solution.py:19
  21.6 47.9 %copy-start.4 = (s32[512]{0:T(512)}, s32[512]{0:T(512)S(1)}, u32[]{:S(2)}) copy-start(s32[512]{0:T(512)S(1)} %pad_add_fusion) | copy-start | bytes 6148
  28.6 16.3 %copy-start.10 = (bf16[64,4096]{1,0:T(8,128)(2,1)}, bf16[64,4096]{1,0:T(8,128)(2,1)S(1)}, u32[]{:S(2)}) copy-start(bf16[64,4096]{1,0:T(8,128)(2,1)S(1)} %collective-permute-done) | copy-start | bytes 1572868
  31.7 0.8 copy-start.11
  31.7 18.6 %copy-start.7 = (bf16[256,4096]{1,0:T(8,128)(2,1)}, bf16[256,4096]{1,0:T(8,128)(2,1)S(1)}, u32[]{:S(2)}) copy-start(bf16[256,4096]{1,0:T(8,128)(2,1)S(1)} %collective-permute-done.2.other_ref) | copy-start | bytes 6291460
  32.5 12.4 %collective-permute-start.5 = (bf16[64,4096]{1,0:T(8,128)(2,1)S(1)}, bf16[64,4096]{1,0:T(8,128)(2,1)}, u32[]{:S(2)}, u32[]{:S(2)}) collective-permute-start(bf16[64,4096]{1,0:T(8,128)(2,1)S(1)} %collective-permute-done), channel_id=1, source_target_pairs={{0,224},{32,0},{64,32},{96,64},{128,96},{160,128},{192,160},{224,1... | collective-permute-start | bytes 1572872 | tf_op jit(solution)/shard_map/ppermute | solution.py:15
  32.7 13.7 %collective-permute-start.6 = (bf16[64,4096]{1,0:T(8,128)(2,1)}, bf16[64,4096]{1,0:T(8,128)(2,1)S(1)}, u32[]{:S(2)}, u32[]{:S(2)}) collective-permute-start(bf16[64,4096]{1,0:T(8,128)(2,1)} %copy-done.11), channel_id=1, source_target_pairs={{0,32},{32,64},{64,96},{96,128},{128,160},{160,192},{192,224},{224... | collective-permute-start | bytes 1572872 | tf_op jit(solution)/shard_map/ppermute | solution.py:15
  34.2 35.3 %copy-start.3 = (s32[512,1]{1,0:T(8,128)}, s32[512,1]{1,0:T(8,128)S(1)}, u32[]{:S(2)}) copy-start(s32[512,1]{1,0:T(8,128)S(1)} %add.165.names_ref) | copy-start | bytes 6148
  35.1 13.6 %copy-start.12 = (bf16[64,4096]{1,0:T(8,128)(2,1)S(1)}, bf16[64,4096]{1,0:T(8,128)(2,1)}, u32[]{:S(2)}) copy-start(bf16[64,4096]{1,0:T(8,128)(2,1)} %copy-done.11) | copy-start | bytes 1572868
  36.6 13.7 %copy-start.6 = (bf16[512,4096]{1,0:T(8,128)(2,1)S(1)}, bf16[512,4096]{1,0:T(8,128)(2,1)}, u32[]{:S(2)}) copy-start(bf16[512,4096]{1,0:T(8,128)(2,1)} %constant_dynamic-update-slice_fusion) | copy-start | bytes 12582916
  46.4 0.8 copy-start.8
  47.2 11.7 %collective-permute-start.7 = (bf16[64,4096]{1,0:T(8,128)(2,1)}, bf16[64,4096]{1,0:T(8,128)(2,1)S(1)}, u32[]{:S(2)}, u32[]{:S(2)}) collective-permute-start(bf16[64,4096]{1,0:T(8,128)(2,1)} %collective-permute-done.5), channel_id=1, source_target_pairs={{0,224},{32,0},{64,32},{96,64},{128,96},{160,128},{192,160},{224,1... | collective-permute-start | bytes 1572872 | tf_op jit(solution)/shard_map/ppermute | solution.py:15
  47.4 12.9 %collective-permute-start.8 = (bf16[64,4096]{1,0:T(8,128)(2,1)}, bf16[64,4096]{1,0:T(8,128)(2,1)S(1)}, u32[]{:S(2)}, u32[]{:S(2)}) collective-permute-start(bf16[64,4096]{1,0:T(8,128)(2,1)} %copy-done.8), channel_id=1, source_target_pairs={{0,32},{32,64},{64,96},{96,128},{128,160},{160,192},{192,224},{224... | collective-permute-start | bytes 1572872 | tf_op jit(solution)/shard_map/ppermute | solution.py:15
  50.3 1.4 copy-start.1
  50.3 10.0 %copy-start.9 = (bf16[64,4096]{1,0:T(8,128)(2,1)S(1)}, bf16[64,4096]{1,0:T(8,128)(2,1)}, u32[]{:S(2)}) copy-start(bf16[64,4096]{1,0:T(8,128)(2,1)} %copy-done.8) | copy-start | bytes 1572868
  60.5 5.7 %collective-permute-start.10 = (bf16[32,4096]{1,0:T(8,128)(2,1)S(1)}, bf16[32,4096]{1,0:T(8,128)(2,1)S(1)}, u32[]{:S(2)}, u32[]{:S(2)}) collective-permute-start(bf16[32,4096]{1,0:T(8,128)(2,1)S(1)} %slice.66), channel_id=1, source_target_pairs={{0,224},{32,0},{64,32},{96,64},{128,96},{160,128},{192,160},{224,1... | collective-permute-start | bytes 786440 | tf_op jit(solution)/shard_map/ppermute | solution.py:15
  60.9 7.1 %collective-permute-start.9 = (bf16[32,4096]{1,0:T(8,128)(2,1)S(1)}, bf16[32,4096]{1,0:T(8,128)(2,1)S(1)}, u32[]{:S(2)}, u32[]{:S(2)}) collective-permute-start(bf16[32,4096]{1,0:T(8,128)(2,1)S(1)} %slice.65), channel_id=1, source_target_pairs={{0,32},{32,64},{64,96},{96,128},{128,160},{160,192},{192,224},{224... | collective-permute-start | bytes 786440 | tf_op jit(solution)/shard_map/ppermute | solution.py:15
  69.5 23.6 %copy-start = (f32[512,512]{1,0:T(8,128)}, f32[512,512]{1,0:T(8,128)S(1)}, u32[]{:S(2)}) copy-start(f32[512,512]{1,0:T(8,128)S(1)} %pad_maximum_fusion.2.logits_ref) | copy-start | bytes 3145732
  70.8 19.5 %all-to-all-start = ((f32[32,3,512]{2,1,0:T(4,128)}), f32[32,3,512]{2,1,0:T(4,128)S(1)}, u32[]{:S(2)}, u32[]{:S(2)}) async-start(f32[32,3,512]{2,1,0:T(4,128)} %bitcast.2), calls=%async_computation | async-start | bytes 524288 | tf_op jit(solution)/shard_map/all_to_all | solution.py:153
  81.5 75.0 %reduce-scatter.2.cloned.1.call-start = ((), (), s32[]{:S(2)}) async-start(), calls=%async_computation.5 | async-start | bytes 4718592 | tf_op jit(solution)/shard_map/reduce_scatter | solution.py:200
  107.0 1.0 copy-start.5
  108.1 1.6 copy-start.2
  118.2 4.5 %collective-permute-start.11 = (bf16[4,256,1024]{2,1,0:T(8,128)(2,1)S(1)}, bf16[4,256,1024]{2,1,0:T(8,128)(2,1)S(1)}, u32[]{:S(2)}, u32[]{:S(2)}) collective-permute-start(bf16[4,256,1024]{2,1,0:T(8,128)(2,1)S(1)} %get-tuple-element.17), channel_id=1, source_target_pairs={{0,16},{16,0},{1,17},{17,1},{2,18},{18,2},{3,19},{19,3},{4,20},{20... | collective-permute-start | bytes 6291464 | tf_op jit(solution)/shard_map/ppermute | solution.py:19
  143.1 10.4 %all-to-all-start.2 = ((bf16[4,256,256]{2,1,0:T(8,128)(2,1)}), bf16[4,256,256]{2,1,0:T(8,128)(2,1)S(1)}, u32[]{:S(2)}, u32[]{:S(2)}) async-start(bf16[4,256,256]{2,1,0:T(8,128)(2,1)} %pad_maximum_fusion.4), calls=%async_computation.2 | async-start | bytes 1048576 | tf_op jit(solution)/shard_map/all_to_all | solution.py:36
Sparse Core Ops, SparseCore 0:
  10.6 62.8 all-gather.1
  107.2 49.2 reduce-scatter.1

commit v2 on v1

--- a/solution.py
+++ b/solution.py
@@ -8,6 +8,10 @@
 bf16, f32, i32 = jnp.bfloat16, jnp.float32, jnp.int32
 NX, NY, NZ = 4, 4, 8
 PARAMS = pltpu.CompilerParams(vmem_limit_bytes=40 << 20)
+ANY = pl.BlockSpec(memory_space=pl.ANY)
+VMEM = pl.BlockSpec(memory_space=pltpu.VMEM)
+SMEM = pl.BlockSpec(memory_space=pltpu.SMEM)
+WIDTH = 512
 ALONE = pltpu.CompilerParams(vmem_limit_bytes=60 << 20)
 
 
@@ -51,43 +55,111 @@
     out_ref[2:3] = jnp.sum(jnp.where(hit, logits, 0.0), axis=0, keepdims=True)
 
 
+def columns(ref, i):
+    return ref.at[:, pl.ds(i * WIDTH, WIDTH)]
+
+
+def lookup_body(names_ref, ids_ref, cots_hbm, out_hbm, hits, cots_ref, sums, in_sems, out_sems):
+    steps = out_hbm.shape[1] // WIDTH
+
+    def fetch(i):
+        return pltpu.make_async_copy(columns(cots_hbm, i), columns(cots_ref, i), in_sems.at[i])
+
+    def store(i):
+        return pltpu.make_async_copy(sums.at[i % 2], columns(out_hbm, i), out_sems.at[i % 2])
+
+    for i in range(steps):
+        fetch(i).start()
+    hits[...] = (names_ref[...] == ids_ref[...]).astype(f32).astype(bf16)
+    for i in range(steps):
+        fetch(i).wait()
+        if i >= 2:
+            store(i - 2).wait()
+        cols = slice(i * WIDTH, (i + 1) * WIDTH)
+        term = jnp.dot(hits[...], cots_ref[:, cols], preferred_element_type=f32)
+        sums[i % 2] = term.astype(bf16)
+        store(i).start()
+    store(steps - 2).wait()
+    store(steps - 1).wait()
+
+
 def head_body(
-    starts, logits_ref, names_ref, tokens_ref, wanted_ref, in_order_ref, ids_ref,
-    own_ref, other_ref, cots_ref, out_ref, d_ref, sorted_ref, hits_ref,
+    starts, logits_ref, names_ref, tokens_ref, wanted_ref, own_hbm, other_hbm, looked_hbm,
+    out_hbm, d_ref, sorted_ref, own_ref, other_ref, looked_ref, sums, in_sems, out_sems,
 ):
-    @pl.when(pl.program_id(0) == 0)
-    def _():
-        rows = d_ref.shape[0] // NZ
-        share = jnp.exp(logits_ref[...] - tokens_ref[0:1]) / tokens_ref[1:2]
-        hit = (names_ref[...] == wanted_ref[...]).astype(f32)
-        d_ref[...] = (tokens_ref[2:3] * (share - hit)).astype(bf16)
-        for k in range(NZ):
-            start = pl.multiple_of(starts[k], rows)
-            sorted_ref[pl.ds(start, rows), :] = d_ref[k * rows : (k + 1) * rows]
-        hits_ref[...] = (in_order_ref[...] == ids_ref[...]).astype(f32).astype(bf16)
+    steps = out_hbm.shape[1] // WIDTH
+
+    def fetches(i):
+        pairs = ((own_hbm, own_ref), (other_hbm, other_ref), (looked_hbm, looked_ref))
+        return [
+            pltpu.make_async_copy(columns(src, i), columns(dst, i), in_sems.at[j, i])
+            for j, (src, dst) in enumerate(pairs)
+        ]
+
+    def store(i):
+        return pltpu.make_async_copy(sums.at[i % 2], columns(out_hbm, i), out_sems.at[i % 2])
+
+    for i in range(steps):
+        for fetch in fetches(i):
+            fetch.start()
+    share = jnp.exp(logits_ref[...] - tokens_ref[0:1]) / tokens_ref[1:2]
+    hit = (names_ref[...] == wanted_ref[...]).astype(f32)
+    d_ref[...] = (tokens_ref[2:3] * (share - hit)).astype(bf16)
+    pieces = starts.shape[0]
+    rows = d_ref.shape[0] // pieces
+    for k in range(pieces):
+        start = pl.multiple_of(starts[k], rows)
+        sorted_ref[pl.ds(start, rows), :] = d_ref[k * rows : (k + 1) * rows]
 
     tokens = own_ref.shape[0]
-    term = jnp.dot(hits_ref[...], cots_ref[...], preferred_element_type=f32)
-    term += jnp.dot(sorted_ref[:, :tokens], own_ref[...], preferred_element_type=f32)
-    term += jnp.dot(sorted_ref[:, tokens:], other_ref[...], preferred_element_type=f32)
-    out_ref[...] = term.astype(bf16)
+    for i in range(steps):
+        for fetch in fetches(i):
+            fetch.wait()
+        cols = slice(i * WIDTH, (i + 1) * WIDTH)
+        term = looked_ref[:, cols].astype(f32)
+        term += jnp.dot(sorted_ref[:, :tokens], own_ref[:, cols], preferred_element_type=f32)
+        term += jnp.dot(sorted_ref[:, tokens:], other_ref[:, cols], preferred_element_type=f32)
+        if i >= 2:
+            store(i - 2).wait()
+        sums[i % 2] = term.astype(bf16)
+        store(i).start()
+    store(steps - 2).wait()
+    store(steps - 1).wait()
 
 
 def state_body(order, d_ref, *refs):
-    *table_refs, own_ref, their_ref, turned = refs
-
-    @pl.when(pl.program_id(0) == 0)
-    def _():
-        turned[...] = d_ref[...].astype(f32).T.astype(bf16)
-
-    start, term = 0, 0.0
-    for t_ref in table_refs:
-        stop = start + t_ref.shape[0]
-        term += jnp.dot(turned[:, start:stop], t_ref[...], preferred_element_type=f32)
-        start = stop
-    tokens = own_ref.shape[1]
-    own_ref[0] = term[:tokens].astype(bf16)
-    their_ref[0] = term[tokens:].astype(bf16)
+    n = (len(refs) - 4) // 2
+    table_hbm, own_ref, their_ref, turned = refs[:n], refs[n], refs[n + 1], refs[n + 2]
+    table_refs, sems = refs[n + 3 : -1], refs[-1]
+    tokens, width = own_ref.shape[1], own_ref.shape[2] // 4
+
+    def fetches(i):
+        cols = pl.ds(i * WIDTH, WIDTH)
+        return [
+            pltpu.make_async_copy(src.at[:, cols], dst.at[:, cols], sems.at[j, i])
+            for j, (src, dst) in enumerate(zip(table_hbm, table_refs))
+        ]
+
+    steps = table_hbm[0].shape[1] // WIDTH
+    for i in range(steps):
+        for fetch in fetches(i):
+            fetch.start()
+    turned[...] = d_ref[...].astype(f32).T.astype(bf16)
+    for i in range(steps):
+        for fetch in fetches(i):
+            fetch.wait()
+        start, term = 0, 0.0
+        for t_ref in table_refs:
+            stop = start + t_ref.shape[0]
+            part = t_ref[:, i * WIDTH : (i + 1) * WIDTH]
+            term += jnp.dot(turned[:, start:stop], part, preferred_element_type=f32)
+            start = stop
+        for j in range(WIDTH // width):
+            spot = order[i * (WIDTH // width) + j]
+            one, two = spot // 4, spot % 4
+            block = term[:, j * width : (j + 1) * width].astype(bf16)
+            own_ref[one, :, pl.ds(pl.multiple_of(two * width, width), width)] = block[:tokens]
+            their_ref[two, :, pl.ds(pl.multiple_of(one * width, width), width)] = block[tokens:]
 
 
 def shards(hidden, table, targets, token_scale, enc_ids, enc_cot, dec_ids, dec_cot):
@@ -154,69 +226,64 @@
         stats.reshape((peers,) + stats.shape[2:]), ("c", "x", "y"), 0, 0, tiled=True
     )
 
+    looked_up = pl.pallas_call(
+        lookup_body,
+        out_shape=jax.ShapeDtypeStruct((vocab, depth), bf16),
+        in_specs=[VMEM, VMEM, ANY],
+        out_specs=ANY,
+        scratch_shapes=[
+            pltpu.VMEM((vocab, n_ids), bf16),
+            pltpu.VMEM((n_ids, depth), bf16),
+            pltpu.VMEM((2, vocab, WIDTH), bf16),
+            pltpu.SemaphoreType.DMA((depth // WIDTH,)),
+            pltpu.SemaphoreType.DMA((2,)),
+        ],
+        compiler_params=ALONE,
+        cost_estimate=cost(2 * vocab * n_ids * depth, 2 * n_ids * depth + 2 * vocab * depth),
+        name="lookup",
+    )(in_order, ids, cots)
+    stats, looked_up = lax.optimization_barrier((stats, looked_up))
     row_max = jnp.max(stats[:, 0], axis=0)
     row_sum = jnp.sum(stats[:, 1] * jnp.exp(stats[:, 0] - row_max), axis=0)
     loss = row_max + jnp.log(row_sum) - jnp.sum(stats[:, 2], axis=0)
 
-    width = 512
     head, dlogits = pl.pallas_call(
         head_body,
         out_shape=(
             jax.ShapeDtypeStruct((vocab, depth), bf16),
             jax.ShapeDtypeStruct((vocab, 2 * tokens), bf16),
         ),
-        grid_spec=pltpu.PrefetchScalarGridSpec(
-            num_scalar_prefetch=1,
-            grid=(depth // width,),
-            in_specs=[
-                pl.BlockSpec((vocab, 2 * tokens), lambda i, s: (0, 0)),
-                pl.BlockSpec((vocab, 1), lambda i, s: (0, 0)),
-                pl.BlockSpec((3, 2 * tokens), lambda i, s: (0, 0)),
-                pl.BlockSpec((1, 2 * tokens), lambda i, s: (0, 0)),
-                pl.BlockSpec((vocab, 1), lambda i, s: (0, 0)),
-                pl.BlockSpec((1, n_ids), lambda i, s: (0, 0)),
-                pl.BlockSpec((tokens, width), lambda i, s: (0, i)),
-                pl.BlockSpec((tokens, width), lambda i, s: (0, i)),
-                pl.BlockSpec((n_ids, width), lambda i, s: (0, i)),
-            ],
-            out_specs=(
-                pl.BlockSpec((vocab, width), lambda i, s: (0, i)),
-                pl.BlockSpec((vocab, 2 * tokens), lambda i, s: (0, 0)),
-            ),
-            scratch_shapes=[
-                pltpu.VMEM((vocab, 2 * tokens), bf16),
-                pltpu.VMEM((vocab, n_ids), bf16),
-            ],
-        ),
+        in_specs=[SMEM] + [VMEM] * 4 + [ANY] * 3,
+        out_specs=(ANY, VMEM),
+        scratch_shapes=[
+            pltpu.VMEM((vocab, 2 * tokens), bf16),
+            pltpu.VMEM((tokens, depth), bf16),
+            pltpu.VMEM((tokens, depth), bf16),
+            pltpu.VMEM((vocab, depth), bf16),
+            pltpu.VMEM((2, vocab, WIDTH), bf16),
+            pltpu.SemaphoreType.DMA((3, depth // WIDTH)),
+            pltpu.SemaphoreType.DMA((2,)),
+        ],
         compiler_params=ALONE,
-        cost_estimate=cost(
-            2 * vocab * (2 * tokens + n_ids) * depth, 2 * (vocab + 2 * tokens + n_ids) * depth
-        ),
+        cost_estimate=cost(4 * vocab * tokens * depth, 4 * vocab * depth + 4 * tokens * depth),
         name="head",
     )(
         places * rows, logits, names, jnp.concatenate([row_max[None], row_sum[None], scales]),
-        wanted, in_order, ids, hidden, other, cots,
+        wanted, hidden, other, looked_up,
     )
     grad_table = lax.psum_scatter(head, "z", scatter_dimension=0, tiled=True).astype(f32)
 
     width = depth // (NX * NY)
     spot = jnp.arange(NX * NY, dtype=i32)
     spot = jnp.where(c == 0, spot, spot % 4 * 4 + spot // 4)
-    out = pl.BlockSpec((1, tokens, width), lambda i, order: (i // 4, 0, i % 4))
-    given = pl.BlockSpec((1, tokens, width), lambda i, order: (i % 4, 0, i // 4))
     own, theirs = pl.pallas_call(
         state_body,
         out_shape=(jax.ShapeDtypeStruct((4, tokens, depth // 4), bf16),) * 2,
-        grid_spec=pltpu.PrefetchScalarGridSpec(
-            num_scalar_prefetch=1,
-            grid=(NX * NY,),
-            in_specs=[
-                pl.BlockSpec((vocab, 2 * tokens), lambda i, order: (0, 0)),
-            ]
-            + [pl.BlockSpec((p.shape[0], width), lambda i, order: (0, order[i])) for p in parts],
-            out_specs=(out, given),
-            scratch_shapes=[pltpu.VMEM((2 * tokens, vocab), bf16)],
-        ),
+        in_specs=[SMEM, VMEM] + [ANY] * len(parts),
+        out_specs=(VMEM, VMEM),
+        scratch_shapes=[pltpu.VMEM((2 * tokens, vocab), bf16)]
+        + [pltpu.VMEM(part.shape, bf16) for part in parts]
+        + [pltpu.SemaphoreType.DMA((len(parts), depth // WIDTH))],
         compiler_params=PARAMS,
         cost_estimate=cost(4 * vocab * tokens * depth, 2 * (vocab + 2 * tokens) * depth),
         name="state_terms",

time: 166 us -> 163 us (0.982)
  waiting for transfers between devices: 53.2 us -> 49.1 us
  local copies, waits for them, and re-layouts: 11.6 us -> 9.85 us
    pallas_call x0 -> x1, Pallas kernels: none -> 9.14 us  [shards(): pl.pallas_call(lookup_body, out_shape=jax.ShapeDtypeStruct((vocab, depth)...]
    all_to_all x1, waiting for transfers between devices: 8.26 us -> 0.01 us  [shards(): lax.all_to_all(stats.reshape((peers,) + stats.shape[2:]), ('c', 'x', 'y')...]
    pallas_call x1, Pallas kernels: 13.9 us -> 8.34 us  [shards(): pl.pallas_call(head_body, out_shape=(jax.ShapeDtypeStruct((vocab, depth),...]
    reduce_scatter x1, waiting for transfers between devices: 2.2 us -> 6.59 us  [shards(): lax.psum_scatter(head, 'z', scatter_dimension=0, tiled=True).astype(f32)]
    pallas_call x1, Pallas kernels: 8.51 us -> 6.18 us  [shards(): pl.pallas_call(state_body, out_shape=(jax.ShapeDtypeStruct((4, tokens, de...]
    unnamed x31 -> x23, local copies, waits for them, and re-layouts: 7.59 us -> 5.82 us
  transfers between devices with their start and end apart: 16 -> 16, of which waited for: 12 -> 10; matrix products, arithmetic and copies ran while one was open for 11% -> 12% of each run, Pallas kernels for 5% -> 10%
where the time goes in v2:
time: 163 us; the launch traced here: 162 us
  waiting for transfers between devices  49.1 us (30%)
  starting transfers between devices  28 us (17%)
  Pallas kernels  24 us (15%)
  blocking collectives  19.3 us (12%)
  between operations  14.4 us (9%)
  other arithmetic  13.6 us (8%)
  local copies, waits for them, and re-layouts  9.85 us (6%)
  matrix products  4.21 us (3%)
    ppermute x8, waiting for transfers between devices, shift(): return lax.ppermute(x, 'z', [(i, (i + k) % NZ) for i in range(NZ)])  32.2 us
    all_to_all x1, blocking collectives, exchange(): lax.all_to_all(x, ('c', 'x', 'y'), 0, 0, axis_index_groups=legs(leg), til...  19.3 us
    all_to_all x1, starting transfers between devices, shards(): lax.all_to_all(stats.reshape((peers,) + stats.shape[2:]), ('c', 'x', 'y')...  10.7 us
    pallas_call x1, Pallas kernels, shards(): pl.pallas_call(lookup_body, out_shape=jax.ShapeDtypeStruct((vocab, depth)...  9.14 us
    ppermute x8, starting transfers between devices, shift(): return lax.ppermute(x, 'z', [(i, (i + k) % NZ) for i in range(NZ)])  9.05 us
    pallas_call x1, Pallas kernels, shards(): pl.pallas_call(head_body, out_shape=(jax.ShapeDtypeStruct((vocab, depth),...  8.34 us
    reduce_scatter x1, waiting for transfers between devices, shards(): lax.psum_scatter(head, 'z', scatter_dimension=0, tiled=True).astype(f32)  6.59 us
    all_to_all x1, waiting for transfers between devices, exchange(): lax.all_to_all(x, ('c', 'x', 'y'), 0, 0, axis_index_groups=legs(leg), til...  6.36 us
  transfers between devices with their start and end apart: 16, of which 10 were waited for; matrix products, arithmetic and copies ran while one was open for 12% of the time, Pallas kernels for 10%

profile of v2, /device:TPU:1, one launch (start us, length us, event | category | flops | bytes accessed | tf_op | source)
XLA Modules:
  0.0 162.4 jit_solution(13700587174620166496)
XLA Ops:
  7.2 0.0 all-gather.2.cloned.1.call-start
  7.2 0.8 and_select_fusion.1
  8.0 0.1 select_convert_fusion
  8.1 1.7 %pad_maximum_fusion.5 = bf16[32,4224]{1,0:T(8,128)(2,1)} fusion(bf16[32,128]{1,0:T(8,128)(2,1)S(1)} %select_convert_fusion, bf16[16,4096]{1,0:T(8,128)(2,1)} %param.16, bf16[16,4096]{1,0:T(8,128)(2,1)} %param.14), kind=kLoop, calls=%fused_computation.9 | loop fusion | flops 811008 | bytes 540672 | tf_op jit(solution)/shard_map/concatenate | solution.py:178
  9.8 3.3 %collective-permute-start.2 = (bf16[256,4096]{1,0:T(8,128)(2,1)}, bf16[256,4096]{1,0:T(8,128)(2,1)S(1)}, u32[]{:S(2)}, u32[]{:S(2)}) collective-permute-start(bf16[256,4096]{1,0:T(8,128)(2,1)} %own_hbm.1), channel_id=1, source_target_pairs={{0,16},{16,0},{1,17},{17,1},{2,18},{18,2},{3,19},{19,3},{4,20},{20... | collective-permute-start | bytes 6291464 | tf_op jit(solution)/shard_map/ppermute | solution.py:23
  13.1 3.9 %collective-permute-start = (bf16[64,4096]{1,0:T(8,128)(2,1)}, bf16[64,4096]{1,0:T(8,128)(2,1)}, u32[]{:S(2)}, u32[]{:S(2)}) collective-permute-start(bf16[64,4096]{1,0:T(8,128)(2,1)} %param.10), channel_id=1, source_target_pairs={{0,224},{32,0},{64,32},{96,64},{128,96},{160,128},{192,160},{224,1... | collective-permute-start | bytes 1572872 | tf_op jit(solution)/shard_map/ppermute | solution.py:19
  17.0 0.4 collective-permute-start.3
  17.3 0.2 collective-permute-start.4
  17.5 0.7 multiply_add_fusion.1
  18.2 0.1 iota_add_fusion.1
  18.2 3.2 %constant_dynamic-update-slice_fusion.1 = bf16[512,4096]{1,0:T(8,128)(2,1)} fusion(bf16[256,4096]{1,0:T(8,128)(2,1)} %own_hbm.1), kind=kLoop, calls=%fused_computation.26 | loop fusion | bytes 4194304
  21.4 0.1 iota_add_fusion
  21.5 0.5 broadcast_multiply_fusion.starts
  22.1 6.5 %collective-permute-done = bf16[64,4096]{1,0:T(8,128)(2,1)} collective-permute-done((bf16[64,4096]{1,0:T(8,128)(2,1)}, bf16[64,4096]{1,0:T(8,128)(2,1)}, u32[]{:S(2)}, u32[]{:S(2)}) %collective-permute-start) | collective-permute-done | bytes 524320 | tf_op jit(solution)/shard_map/ppermute | solution.py:19
  28.6 3.1 %collective-permute-done.1 = bf16[64,4096]{1,0:T(8,128)(2,1)} collective-permute-done((bf16[64,4096]{1,0:T(8,128)(2,1)}, bf16[64,4096]{1,0:T(8,128)(2,1)}, u32[]{:S(2)}, u32[]{:S(2)}) %collective-permute-start.1) | collective-permute-done | bytes 524320 | tf_op jit(solution)/shard_map/ppermute | solution.py:19
  31.7 0.4 collective-permute-start.5
  32.1 1.1 collective-permute-start.6
  33.1 0.2 add.165.names_ref
  33.4 0.9 add.164.names_ref
  34.2 1.5 constant_dynamic-update-slice_fusion
  35.7 8.5 %collective-permute-done.5 = bf16[64,4096]{1,0:T(8,128)(2,1)} collective-permute-done((bf16[64,4096]{1,0:T(8,128)(2,1)}, bf16[64,4096]{1,0:T(8,128)(2,1)}, u32[]{:S(2)}, u32[]{:S(2)}) %collective-permute-start.5) | collective-permute-done | bytes 524320 | tf_op jit(solution)/shard_map/ppermute | solution.py:19
  44.2 1.5 collective-permute-done.6
  45.8 0.4 collective-permute-start.7
  46.2 1.1 collective-permute-start.8
  47.2 1.6 pad_maximum_fusion.refs_0_
  48.9 1.3 fusion.7
  50.2 7.3 %collective-permute-done.7 = bf16[64,4096]{1,0:T(8,128)(2,1)S(1)} collective-permute-done((bf16[64,4096]{1,0:T(8,128)(2,1)}, bf16[64,4096]{1,0:T(8,128)(2,1)S(1)}, u32[]{:S(2)}, u32[]{:S(2)}) %collective-permute-start.7) | collective-permute-done | bytes 524320 | tf_op jit(solution)/shard_map/ppermute | solution.py:19
  57.4 2.0 %collective-permute-start.10 = (bf16[32,4096]{1,0:T(8,128)(2,1)S(1)}, bf16[32,4096]{1,0:T(8,128)(2,1)S(1)}, u32[]{:S(2)}, u32[]{:S(2)}) collective-permute-start(bf16[32,4096]{1,0:T(8,128)(2,1)S(1)} %slice.66), channel_id=1, source_target_pairs={{0,224},{32,0},{64,32},{96,64},{128,96},{160,128},{192,160},{224,1... | collective-permute-start | bytes 786440 | tf_op jit(solution)/shard_map/ppermute | solution.py:19
  59.5 0.1 pad_maximum_fusion.1.refs_1_
  59.6 0.3 collective-permute-start.9
  59.9 1.5 fusion.8
  61.4 1.8 %collective-permute-done.10 = bf16[32,4096]{1,0:T(8,128)(2,1)S(1)} collective-permute-done((bf16[32,4096]{1,0:T(8,128)(2,1)S(1)}, bf16[32,4096]{1,0:T(8,128)(2,1)S(1)}, u32[]{:S(2)}, u32[]{:S(2)}) %collective-permute-start.10) | collective-permute-done | bytes 262176 | tf_op jit(solution)/shard_map/ppermute | solution.py:19
  63.1 3.5 %collective-permute-done.9 = bf16[32,4096]{1,0:T(8,128)(2,1)S(1)} collective-permute-done((bf16[32,4096]{1,0:T(8,128)(2,1)S(1)}, bf16[32,4096]{1,0:T(8,128)(2,1)S(1)}, u32[]{:S(2)}, u32[]{:S(2)}) %collective-permute-start.9) | collective-permute-done | bytes 262176 | tf_op jit(solution)/shard_map/ppermute | solution.py:19
  66.7 1.4 fusion.9
  68.1 0.1 pad_maximum_fusion.2.logits_ref
  68.2 0.4 stats.1
  68.6 0.1 broadcast_select_fusion
  68.7 0.7 broadcast_in_dim.76
  69.4 10.7 %all-to-all-start = ((f32[32,3,512]{2,1,0:T(4,128)}), f32[32,3,512]{2,1,0:T(4,128)S(1)}, u32[]{:S(2)}, u32[]{:S(2)}) async-start(f32[32,3,512]{2,1,0:T(4,128)} %bitcast.32), calls=%async_computation | async-start | bytes 524288 | tf_op jit(solution)/shard_map/all_to_all | solution.py:225
  80.2 0.0 reduce-scatter.2.cloned.1.call-start
  80.2 0.0 all-gather.2.cloned.1.call-done.cots_hbm
  80.2 1.0 slice_convert_fusion
  81.2 1.0 fusion
  82.2 9.1 %lookup.1.looked_hbm = bf16[512,4096]{1,0:T(8,128)(2,1)} custom-call(s32[512,1]{1,0:T(8,128)} %add.164.names_ref, s32[1,1024]{1,0:T(1,128)} %bitcast.36, bf16[1024,4224]{1,0:T(8,128)(2,1)} %all-gather.2.cloned.1.call-done.cots_hbm), custom_call_target="tpu_custom_call" | custom-call | flops 4294967296 | bytes 12582912 | tf_op jit(solution)/shard_map/lookup/pallas_call | solution.py:229
  91.4 0.1 slice_reduce_fusion
  91.5 0.1 copy.22
  91.6 0.6 pad_maximum_fusion.7.tokens_ref
  92.2 8.3 %head.1 = (bf16[512,4096]{1,0:T(8,128)(2,1)}, bf16[512,512]{1,0:T(8,128)(2,1)}) custom-call(s32[8]{0:T(128)} %broadcast_multiply_fusion.starts, f32[512,512]{1,0:T(8,128)} %copy-done, s32[512,1]{1,0:T(8,128)} %copy-done.1, f32[3,512]{1,0:T(4,128)} %pad_maximum_fusion.7.tokens_ref, s32[1,512]{1,0:T(1,128)} %bitcast.31, bf16[256,4096]{1,0:T(8,128)(2,1)} %own_hbm.1, ...), custom_call_target="tpu_custom_call" | custom-call | flops 2147483648 | bytes 12582912 | tf_op jit(solution)/shard_map/head/pallas_call | solution.py:250
  100.6 0.0 reduce-scatter.2.cloned.1.call-update
  100.6 1.0 copy-done.5
  101.6 1.6 copy-done.3
  103.2 6.2 %state_terms.1 = (bf16[4,256,1024]{2,1,0:T(8,128)(2,1)S(1)}, bf16[4,256,1024]{2,1,0:T(8,128)(2,1)S(1)}) custom-call(s32[16]{0:T(128)S(1)} %broadcast_select_fusion.1.order, bf16[512,512]{1,0:T(8,128)(2,1)S(1)} %copy-done.5, bf16[256,4096]{1,0:T(8,128)(2,1)S(1)} %copy-done.3, bf16[192,4096]{1,0:T(8,128)(2,1)S(1)} %pad_maximum_fusion.1.refs_1_, ...), custom_call_target="tpu_custom_call" | custom-call | flops 2147483648 | bytes 8388608 | tf_op jit(solution)/shard_map/state_terms/pallas_call | solution.py:279
  109.4 0.3 collective-permute-start.11
  109.7 3.9 %collective-permute-done.11 = bf16[4,256,1024]{2,1,0:T(8,128)(2,1)S(1)} collective-permute-done((bf16[4,256,1024]{2,1,0:T(8,128)(2,1)S(1)}, bf16[4,256,1024]{2,1,0:T(8,128)(2,1)S(1)}, u32[]{:S(2)}, u32[]{:S(2)}) %collective-permute-start.11) | collective-permute-done | bytes 2097184 | tf_op jit(solution)/shard_map/ppermute | solution.py:23
  113.7 1.0 add_convert_fusion
  114.6 19.3 %all_to_all.15 = bf16[4,256,1024]{2,1,0:T(8,128)(2,1)S(1)} all-to-all(bf16[4,256,1024]{2,1,0:T(8,128)(2,1)S(1)} %add_convert_fusion), channel_id=1, replica_groups={{0,4,8,12},{1,5,9,13},{2,6,10,14},{3,7,11,15},{16,17,18,19},{20,21,22,2..., dimensions={0} | all-to-all | bytes 4194304 | tf_op jit(solution)/shard_map/all_to_all | solution.py:40
  133.9 0.4 reduce.3
  134.4 0.9 pad_maximum_fusion.4
  135.3 4.0 %all-to-all-start.2 = ((bf16[4,256,256]{2,1,0:T(8,128)(2,1)}), bf16[4,256,256]{2,1,0:T(8,128)(2,1)S(1)}, u32[]{:S(2)}, u32[]{:S(2)}) async-start(bf16[4,256,256]{2,1,0:T(8,128)(2,1)} %pad_maximum_fusion.4), calls=%async_computation.2 | async-start | bytes 1048576 | tf_op jit(solution)/shard_map/all_to_all | solution.py:40
  139.2 0.6 slice.64
  139.8 6.4 %all-to-all-done.2 = bf16[4,256,256]{2,1,0:T(8,128)(2,1)S(1)} async-done(((bf16[4,256,256]{2,1,0:T(8,128)(2,1)}), bf16[4,256,256]{2,1,0:T(8,128)(2,1)S(1)}, u32[]{:S(2)}, u32[]{:S(2)}) %all-to-all-start.2) | async-done | bytes 524320 | tf_op jit(solution)/shard_map/all_to_all | solution.py:40
  146.2 0.7 reduce_sum.41
  146.9 6.6 %reduce-scatter.2.cloned.1.call-done = bf16[64,4096]{1,0:T(8,128)(2,1)} async-done(((bf16[512,4096]{1,0:T(8,128)(2,1)}), bf16[64,4096]{1,0:T(8,128)(2,1)}) %reduce-scatter.2.cloned.1.call-update) | async-done | bytes 524304 | tf_op jit(solution)/shard_map/reduce_scatter | solution.py:274
  153.5 2.1 %convert_element_type.30 = f32[64,4096]{1,0:T(8,128)} convert(bf16[64,4096]{1,0:T(8,128)(2,1)} %reduce-scatter.2.cloned.1.call-done) | non-fusion elementwise | flops 262144 | bytes 1572864 | tf_op jit(solution)/shard_map/convert_element_type | solution.py:274
  (42 shorter events, 0.3 us)
Async XLA Ops:
  7.2 14.9 %copy-start.9 = (s32[256]{0:T(256)S(1)}, s32[256]{0:T(256)}, u32[]{:S(2)}) copy-start(s32[256]{0:T(256)} %param.11) | copy-start | bytes 3076
  7.2 14.9 %copy-start.10 = (f32[256]{0:T(256)S(1)}, f32[256]{0:T(256)}, u32[]{:S(2)}) copy-start(f32[256]{0:T(256)} %param.12) | copy-start | bytes 3076
  7.2 73.0 %all-gather.2.cloned.1.call-start = ((), (), s32[]{:S(2)}) async-start(), calls=%async_computation.4 | async-start | bytes 8921088 | tf_op jit(solution)/shard_map/all_gather | solution.py:179
  9.8 21.9 %collective-permute-start.2 = (bf16[256,4096]{1,0:T(8,128)(2,1)}, bf16[256,4096]{1,0:T(8,128)(2,1)S(1)}, u32[]{:S(2)}, u32[]{:S(2)}) collective-permute-start(bf16[256,4096]{1,0:T(8,128)(2,1)} %own_hbm.1), channel_id=1, source_target_pairs={{0,16},{16,0},{1,17},{17,1},{2,18},{18,2},{3,19},{19,3},{4,20},{20... | collective-permute-start | bytes 6291464 | tf_op jit(solution)/shard_map/ppermute | solution.py:23
  13.1 15.4 %collective-permute-start = (bf16[64,4096]{1,0:T(8,128)(2,1)}, bf16[64,4096]{1,0:T(8,128)(2,1)}, u32[]{:S(2)}, u32[]{:S(2)}) collective-permute-start(bf16[64,4096]{1,0:T(8,128)(2,1)} %param.10), channel_id=1, source_target_pairs={{0,224},{32,0},{64,32},{96,64},{128,96},{160,128},{192,160},{224,1... | collective-permute-start | bytes 1572872 | tf_op jit(solution)/shard_map/ppermute | solution.py:19
  17.0 14.7 %collective-permute-start.1 = (bf16[64,4096]{1,0:T(8,128)(2,1)}, bf16[64,4096]{1,0:T(8,128)(2,1)}, u32[]{:S(2)}, u32[]{:S(2)}) collective-permute-start(bf16[64,4096]{1,0:T(8,128)(2,1)} %param.10), channel_id=1, source_target_pairs={{0,32},{32,64},{64,96},{96,128},{128,160},{160,192},{192,224},{224... | collective-permute-start | bytes 1572872 | tf_op jit(solution)/shard_map/ppermute | solution.py:19
  17.0 5.0 %collective-permute-start.3 = (s32[256]{0:T(256)}, s32[256]{0:T(256)S(1)}, u32[]{:S(2)}, u32[]{:S(2)}) collective-permute-start(s32[256]{0:T(256)} %param.11), channel_id=1, source_target_pairs={{0,16},{16,0},{1,17},{17,1},{2,18},{18,2},{3,19},{19,3},{4,20},{20... | collective-permute-start | bytes 3080 | tf_op jit(solution)/shard_map/ppermute | solution.py:23
  17.3 4.7 %collective-permute-start.4 = (f32[256]{0:T(256)}, f32[256]{0:T(256)S(1)}, u32[]{:S(2)}, u32[]{:S(2)}) collective-permute-start(f32[256]{0:T(256)} %param.12), channel_id=1, source_target_pairs={{0,16},{16,0},{1,17},{17,1},{2,18},{18,2},{3,19},{19,3},{4,20},{20... | collective-permute-start | bytes 3080 | tf_op jit(solution)/shard_map/ppermute | solution.py:23
  21.4 25.8 %copy-start.8 = (bf16[64,4096]{1,0:T(8,128)(2,1)S(1)}, bf16[64,4096]{1,0:T(8,128)(2,1)}, u32[]{:S(2)}) copy-start(bf16[64,4096]{1,0:T(8,128)(2,1)} %param.10) | copy-start | bytes 1572868
  22.0 46.2 %copy-start.4 = (s32[512]{0:T(512)}, s32[512]{0:T(512)S(1)}, u32[]{:S(2)}) copy-start(s32[512]{0:T(512)S(1)} %pad_add_fusion) | copy-start | bytes 6148
  31.7 17.2 %copy-start.7 = (bf16[256,4096]{1,0:T(8,128)(2,1)}, bf16[256,4096]{1,0:T(8,128)(2,1)S(1)}, u32[]{:S(2)}) copy-start(bf16[256,4096]{1,0:T(8,128)(2,1)S(1)} %collective-permute-done.2.other_hbm) | copy-start | bytes 6291460
  31.7 12.5 %collective-permute-start.5 = (bf16[64,4096]{1,0:T(8,128)(2,1)}, bf16[64,4096]{1,0:T(8,128)(2,1)}, u32[]{:S(2)}, u32[]{:S(2)}) collective-permute-start(bf16[64,4096]{1,0:T(8,128)(2,1)} %collective-permute-done), channel_id=1, source_target_pairs={{0,224},{32,0},{64,32},{96,64},{128,96},{160,128},{192,160},{224,1... | collective-permute-start | bytes 1572872 | tf_op jit(solution)/shard_map/ppermute | solution.py:19
  32.1 13.7 %collective-permute-start.6 = (bf16[64,4096]{1,0:T(8,128)(2,1)}, bf16[64,4096]{1,0:T(8,128)(2,1)S(1)}, u32[]{:S(2)}, u32[]{:S(2)}) collective-permute-start(bf16[64,4096]{1,0:T(8,128)(2,1)} %collective-permute-done.1), channel_id=1, source_target_pairs={{0,32},{32,64},{64,96},{96,128},{128,160},{160,192},{192,224},{224... | collective-permute-start | bytes 1572872 | tf_op jit(solution)/shard_map/ppermute | solution.py:19
  33.3 34.9 %copy-start.1 = (s32[512,1]{1,0:T(8,128)}, s32[512,1]{1,0:T(8,128)S(1)}, u32[]{:S(2)}) copy-start(s32[512,1]{1,0:T(8,128)S(1)} %add.165.names_ref) | copy-start | bytes 6148
  35.7 13.1 %copy-start.6 = (bf16[512,4096]{1,0:T(8,128)(2,1)S(1)}, bf16[512,4096]{1,0:T(8,128)(2,1)}, u32[]{:S(2)}) copy-start(bf16[512,4096]{1,0:T(8,128)(2,1)} %constant_dynamic-update-slice_fusion) | copy-start | bytes 12582916
  45.8 11.7 %collective-permute-start.7 = (bf16[64,4096]{1,0:T(8,128)(2,1)}, bf16[64,4096]{1,0:T(8,128)(2,1)S(1)}, u32[]{:S(2)}, u32[]{:S(2)}) collective-permute-start(bf16[64,4096]{1,0:T(8,128)(2,1)} %collective-permute-done.5), channel_id=1, source_target_pairs={{0,224},{32,0},{64,32},{96,64},{128,96},{160,128},{192,160},{224,1... | collective-permute-start | bytes 1572872 | tf_op jit(solution)/shard_map/ppermute | solution.py:19
  46.2 13.3 %collective-permute-start.8 = (bf16[64,4096]{1,0:T(8,128)(2,1)S(1)}, bf16[64,4096]{1,0:T(8,128)(2,1)S(1)}, u32[]{:S(2)}, u32[]{:S(2)}) collective-permute-start(bf16[64,4096]{1,0:T(8,128)(2,1)S(1)} %collective-permute-done.6), channel_id=1, source_target_pairs={{0,32},{32,64},{64,96},{96,128},{128,160},{160,192},{192,224},{224... | collective-permute-start | bytes 1572872 | tf_op jit(solution)/shard_map/ppermute | solution.py:19
  48.8 1.3 copy-start.2
  57.4 5.7 %collective-permute-start.10 = (bf16[32,4096]{1,0:T(8,128)(2,1)S(1)}, bf16[32,4096]{1,0:T(8,128)(2,1)S(1)}, u32[]{:S(2)}, u32[]{:S(2)}) collective-permute-start(bf16[32,4096]{1,0:T(8,128)(2,1)S(1)} %slice.66), channel_id=1, source_target_pairs={{0,224},{32,0},{64,32},{96,64},{128,96},{160,128},{192,160},{224,1... | collective-permute-start | bytes 786440 | tf_op jit(solution)/shard_map/ppermute | solution.py:19
  59.6 7.1 %collective-permute-start.9 = (bf16[32,4096]{1,0:T(8,128)(2,1)S(1)}, bf16[32,4096]{1,0:T(8,128)(2,1)S(1)}, u32[]{:S(2)}, u32[]{:S(2)}) collective-permute-start(bf16[32,4096]{1,0:T(8,128)(2,1)S(1)} %slice.65), channel_id=1, source_target_pairs={{0,32},{32,64},{64,96},{96,128},{128,160},{160,192},{192,224},{224... | collective-permute-start | bytes 786440 | tf_op jit(solution)/shard_map/ppermute | solution.py:19
  68.2 23.1 %copy-start = (f32[512,512]{1,0:T(8,128)}, f32[512,512]{1,0:T(8,128)S(1)}, u32[]{:S(2)}) copy-start(f32[512,512]{1,0:T(8,128)S(1)} %pad_maximum_fusion.2.logits_ref) | copy-start | bytes 3145732
  69.4 21.9 %all-to-all-start = ((f32[32,3,512]{2,1,0:T(4,128)}), f32[32,3,512]{2,1,0:T(4,128)S(1)}, u32[]{:S(2)}, u32[]{:S(2)}) async-start(f32[32,3,512]{2,1,0:T(4,128)} %bitcast.32), calls=%async_computation | async-start | bytes 524288 | tf_op jit(solution)/shard_map/all_to_all | solution.py:225
  80.2 73.4 %reduce-scatter.2.cloned.1.call-start = ((), (), s32[]{:S(2)}) async-start(), calls=%async_computation.5 | async-start | bytes 4718592 | tf_op jit(solution)/shard_map/reduce_scatter | solution.py:274
  100.6 1.0 copy-start.5
  101.6 1.6 copy-start.3
  109.4 4.2 %collective-permute-start.11 = (bf16[4,256,1024]{2,1,0:T(8,128)(2,1)S(1)}, bf16[4,256,1024]{2,1,0:T(8,128)(2,1)S(1)}, u32[]{:S(2)}, u32[]{:S(2)}) collective-permute-start(bf16[4,256,1024]{2,1,0:T(8,128)(2,1)S(1)} %get-tuple-element.21), channel_id=1, source_target_pairs={{0,16},{16,0},{1,17},{17,1},{2,18},{18,2},{3,19},{19,3},{4,20},{20... | collective-permute-start | bytes 6291464 | tf_op jit(solution)/shard_map/ppermute | solution.py:23
  135.3 10.9 %all-to-all-start.2 = ((bf16[4,256,256]{2,1,0:T(8,128)(2,1)}), bf16[4,256,256]{2,1,0:T(8,128)(2,1)S(1)}, u32[]{:S(2)}, u32[]{:S(2)}) async-start(bf16[4,256,256]{2,1,0:T(8,128)(2,1)} %pad_maximum_fusion.4), calls=%async_computation.2 | async-start | bytes 1048576 | tf_op jit(solution)/shard_map/all_to_all | solution.py:40
Sparse Core Ops, SparseCore 0:
  10.6 62.8 all-gather.1
  100.7 52.7 reduce-scatter.1

commit v3 on v2

--- a/solution.py
+++ b/solution.py
@@ -46,6 +46,18 @@
     return pl.CostEstimate(flops=flops, bytes_accessed=moved, transcendentals=0)
 
 
+def gather_body(enc_ids_ref, dec_ids_ref, enc_ref, dec_ref, out_ref):
+    n, depth = enc_ref.shape
+    row = lax.broadcasted_iota(i32, (n, n), 0)
+    same = row == lax.broadcasted_iota(i32, (n, n), 1)
+    lane = lax.broadcasted_iota(i32, (n, 128), 1)
+    for i, (ids_ref, rows_ref) in enumerate(((enc_ids_ref, enc_ref), (dec_ids_ref, dec_ref))):
+        out_ref[i * n : (i + 1) * n, :depth] = rows_ref[...]
+        ids = jnp.sum(jnp.where(same, ids_ref[...], 0), axis=1, keepdims=True)
+        tail = jnp.where(lane == 0, ids >> 7, jnp.where(lane == 1, ids & 127, 0))
+        out_ref[i * n : (i + 1) * n, depth:] = tail.astype(f32).astype(bf16)
+
+
 def stats_body(logits_ref, names_ref, wanted_ref, out_ref):
     logits = logits_ref[...]
     top = jnp.max(logits, axis=0, keepdims=True)
@@ -59,7 +71,7 @@
     return ref.at[:, pl.ds(i * WIDTH, WIDTH)]
 
 
-def lookup_body(names_ref, ids_ref, cots_hbm, out_hbm, hits, cots_ref, sums, in_sems, out_sems):
+def lookup_body(names_ref, cots_hbm, out_hbm, hits, cots_ref, tail_ref, sums, in_sems, out_sems):
     steps = out_hbm.shape[1] // WIDTH
 
     def fetch(i):
@@ -68,9 +80,16 @@
     def store(i):
         return pltpu.make_async_copy(sums.at[i % 2], columns(out_hbm, i), out_sems.at[i % 2])
 
+    tail = pltpu.make_async_copy(
+        cots_hbm.at[:, pl.ds(steps * WIDTH, 128)], tail_ref, in_sems.at[steps]
+    )
+    tail.start()
     for i in range(steps):
         fetch(i).start()
-    hits[...] = (names_ref[...] == ids_ref[...]).astype(f32).astype(bf16)
+    tail.wait()
+    ids = tail_ref[...].astype(f32).T
+    ids = ids[0:1] * 128.0 + ids[1:2]
+    hits[...] = (names_ref[...].astype(f32) == ids).astype(f32).astype(bf16)
     for i in range(steps):
         fetch(i).wait()
         if i >= 2:
@@ -102,7 +121,7 @@
     for i in range(steps):
         for fetch in fetches(i):
             fetch.start()
-    share = jnp.exp(logits_ref[...] - tokens_ref[0:1]) / tokens_ref[1:2]
+    share = jnp.exp(logits_ref[...] - tokens_ref[0:1]) * (1.0 / tokens_ref[1:2])
     hit = (names_ref[...] == wanted_ref[...]).astype(f32)
     d_ref[...] = (tokens_ref[2:3] * (share - hit)).astype(bf16)
     pieces = starts.shape[0]
@@ -170,16 +189,14 @@
     x, y = lax.axis_index("x"), lax.axis_index("y")
     base = (x * NY + y) * (vocab * 2)
 
-    ids = jnp.concatenate([enc_ids, dec_ids])
-    lane = lax.broadcasted_iota(i32, (ids.shape[0], 128), 1)
-    tail = jnp.where(
-        lane == 0, (ids // 128)[:, None], jnp.where(lane == 1, (ids % 128)[:, None], 0)
-    ).astype(bf16)
-    cots = jnp.concatenate([jnp.concatenate([enc_cot, dec_cot], 0), tail], 1)
+    cots = pl.pallas_call(
+        gather_body,
+        out_shape=jax.ShapeDtypeStruct((2 * enc_cot.shape[0], depth + 128), bf16),
+        compiler_params=ALONE,
+        name="id_rows",
+    )(enc_ids[None], dec_ids[None], enc_cot, dec_cot)
     cots = lax.all_gather(cots, ("c", "x", "y"), axis=0, tiled=True)
-    ids = cots[:, depth : depth + 2].astype(i32)
-    ids = (ids[:, 0] * 128 + ids[:, 1])[None]
-    n_ids = ids.shape[1]
+    n_ids = cots.shape[0]
     peers = 2 * NX * NY
 
     half = rows // 2
@@ -229,19 +246,20 @@
     looked_up = pl.pallas_call(
         lookup_body,
         out_shape=jax.ShapeDtypeStruct((vocab, depth), bf16),
-        in_specs=[VMEM, VMEM, ANY],
+        in_specs=[VMEM, ANY],
         out_specs=ANY,
         scratch_shapes=[
             pltpu.VMEM((vocab, n_ids), bf16),
             pltpu.VMEM((n_ids, depth), bf16),
+            pltpu.VMEM((n_ids, 128), bf16),
             pltpu.VMEM((2, vocab, WIDTH), bf16),
-            pltpu.SemaphoreType.DMA((depth // WIDTH,)),
+            pltpu.SemaphoreType.DMA((depth // WIDTH + 1,)),
             pltpu.SemaphoreType.DMA((2,)),
         ],
         compiler_params=ALONE,
         cost_estimate=cost(2 * vocab * n_ids * depth, 2 * n_ids * depth + 2 * vocab * depth),
         name="lookup",
-    )(in_order, ids, cots)
+    )(in_order, cots)
     stats, looked_up = lax.optimization_barrier((stats, looked_up))
     row_max = jnp.max(stats[:, 0], axis=0)
     row_sum = jnp.sum(stats[:, 1] * jnp.exp(stats[:, 0] - row_max), axis=0)

time: 163 us -> 160 us (0.982)
  other arithmetic: 13.6 us -> 9.09 us
  Pallas kernels: 24 us -> 26 us
    pallas_call x0 -> x1, Pallas kernels: none -> 1.8 us  [shards(): pl.pallas_call(gather_body, out_shape=jax.ShapeDtypeStruct((2 * enc_cot.s...]
    concatenate x1 -> x0, other arithmetic: 1.69 us -> none  [shards(): cots = jnp.concatenate([jnp.concatenate([enc_cot, dec_cot], 0), tail], 1)]
  transfers between devices with their start and end apart: 16 -> 16, of which waited for: 10 -> 10; matrix products, arithmetic and copies ran while one was open for 12% -> 11% of each run, Pallas kernels for 10% -> 10%
where the time goes in v3:
time: 160 us
  waiting for transfers between devices  49.1 us (31%)
  starting transfers between devices  28 us (18%)
  Pallas kernels  26 us (16%)
  blocking collectives  19.3 us (12%)
  between operations  14.4 us (9%)
  local copies, waits for them, and re-layouts  9.84 us (6%)
  other arithmetic  9.09 us (6%)
  matrix products  4.2 us (3%)
    ppermute x8, waiting for transfers between devices, shift(): return lax.ppermute(x, 'z', [(i, (i + k) % NZ) for i in range(NZ)])  32.2 us
    all_to_all x1, blocking collectives, exchange(): lax.all_to_all(x, ('c', 'x', 'y'), 0, 0, axis_index_groups=legs(leg), til...  19.3 us
    all_to_all x1, starting transfers between devices, shards(): lax.all_to_all(stats.reshape((peers,) + stats.shape[2:]), ('c', 'x', 'y')...  10.7 us
    pallas_call x1, Pallas kernels, shards(): pl.pallas_call(lookup_body, out_shape=jax.ShapeDtypeStruct((vocab, depth)...  9.24 us
    ppermute x8, starting transfers between devices, shift(): return lax.ppermute(x, 'z', [(i, (i + k) % NZ) for i in range(NZ)])  9.05 us
    pallas_call x1, Pallas kernels, shards(): pl.pallas_call(head_body, out_shape=(jax.ShapeDtypeStruct((vocab, depth),...  8.4 us
    reduce_scatter x1, waiting for transfers between devices, shards(): lax.psum_scatter(head, 'z', scatter_dimension=0, tiled=True).astype(f32)  6.58 us
    all_to_all x1, waiting for transfers between devices, exchange(): lax.all_to_all(x, ('c', 'x', 'y'), 0, 0, axis_index_groups=legs(leg), til...  6.36 us
  transfers between devices with their start and end apart: 16, of which 10 were waited for; matrix products, arithmetic and copies ran while one was open for 11% of the time, Pallas kernels for 10%

profile of v3, /device:TPU:1, one launch (start us, length us, event | category | flops | bytes accessed | tf_op | source)
XLA Modules:
  0.0 159.9 jit_solution(986488461240937402)
XLA Ops:
  7.2 0.0 copy-start.9
  7.2 0.0 copy-start.10
  7.2 0.0 all-gather.2.cloned.1.call-start
  7.2 1.8 %id_rows.1 = bf16[32,4224]{1,0:T(8,128)(2,1)} custom-call(s32[1,16]{1,0:T(1,128)} %bitcast.37, s32[1,16]{1,0:T(1,128)} %bitcast.38, bf16[16,4096]{1,0:T(8,128)(2,1)} %enc_ref.1, bf16[16,4096]{1,0:T(8,128)(2,1)} %dec_ref.1), custom_call_target="tpu_custom_call" | custom-call | tf_op jit(solution)/shard_map/id_rows/pallas_call | solution.py:192
  9.0 0.0 all-gather.2.cloned.1.call-update
  9.1 3.3 %collective-permute-start.2 = (bf16[256,4096]{1,0:T(8,128)(2,1)}, bf16[256,4096]{1,0:T(8,128)(2,1)S(1)}, u32[]{:S(2)}, u32[]{:S(2)}) collective-permute-start(bf16[256,4096]{1,0:T(8,128)(2,1)} %own_hbm.1), channel_id=1, source_target_pairs={{0,16},{16,0},{1,17},{17,1},{2,18},{18,2},{3,19},{19,3},{4,20},{20... | collective-permute-start | bytes 6291464 | tf_op jit(solution)/shard_map/ppermute | solution.py:23
  12.4 3.9 %collective-permute-start = (bf16[64,4096]{1,0:T(8,128)(2,1)}, bf16[64,4096]{1,0:T(8,128)(2,1)}, u32[]{:S(2)}, u32[]{:S(2)}) collective-permute-start(bf16[64,4096]{1,0:T(8,128)(2,1)} %param.10), channel_id=1, source_target_pairs={{0,224},{32,0},{64,32},{96,64},{128,96},{160,128},{192,160},{224,1... | collective-permute-start | bytes 1572872 | tf_op jit(solution)/shard_map/ppermute | solution.py:19
  16.2 0.4 collective-permute-start.3
  16.6 0.2 collective-permute-start.4
  16.8 0.7 multiply_add_fusion.1
  17.4 0.1 iota_add_fusion.1
  17.5 3.2 %constant_dynamic-update-slice_fusion.1 = bf16[512,4096]{1,0:T(8,128)(2,1)} fusion(bf16[256,4096]{1,0:T(8,128)(2,1)} %own_hbm.1), kind=kLoop, calls=%fused_computation.20 | loop fusion | bytes 4194304
  20.7 0.1 iota_add_fusion
  20.8 0.5 broadcast_multiply_fusion.starts
  21.3 6.5 %collective-permute-done = bf16[64,4096]{1,0:T(8,128)(2,1)} collective-permute-done((bf16[64,4096]{1,0:T(8,128)(2,1)}, bf16[64,4096]{1,0:T(8,128)(2,1)}, u32[]{:S(2)}, u32[]{:S(2)}) %collective-permute-start) | collective-permute-done | bytes 524320 | tf_op jit(solution)/shard_map/ppermute | solution.py:19
  27.8 3.1 %collective-permute-done.1 = bf16[64,4096]{1,0:T(8,128)(2,1)} collective-permute-done((bf16[64,4096]{1,0:T(8,128)(2,1)}, bf16[64,4096]{1,0:T(8,128)(2,1)}, u32[]{:S(2)}, u32[]{:S(2)}) %collective-permute-start.1) | collective-permute-done | bytes 524320 | tf_op jit(solution)/shard_map/ppermute | solution.py:19
  30.9 0.4 collective-permute-start.5
  31.3 1.1 collective-permute-start.6
  32.4 0.2 add.134.names_ref
  32.6 0.9 add.133.names_ref
  33.5 1.5 constant_dynamic-update-slice_fusion
  35.0 8.5 %collective-permute-done.5 = bf16[64,4096]{1,0:T(8,128)(2,1)} collective-permute-done((bf16[64,4096]{1,0:T(8,128)(2,1)}, bf16[64,4096]{1,0:T(8,128)(2,1)}, u32[]{:S(2)}, u32[]{:S(2)}) %collective-permute-start.5) | collective-permute-done | bytes 524320 | tf_op jit(solution)/shard_map/ppermute | solution.py:19
  43.5 1.5 collective-permute-done.6
  45.0 0.4 collective-permute-start.7
  45.4 1.1 collective-permute-start.8
  46.5 1.6 pad_maximum_fusion.refs_0_
  48.1 1.3 fusion.6
  49.4 0.0 copy-done.2
  49.4 7.3 %collective-permute-done.7 = bf16[64,4096]{1,0:T(8,128)(2,1)S(1)} collective-permute-done((bf16[64,4096]{1,0:T(8,128)(2,1)}, bf16[64,4096]{1,0:T(8,128)(2,1)S(1)}, u32[]{:S(2)}, u32[]{:S(2)}) %collective-permute-start.7) | collective-permute-done | bytes 524320 | tf_op jit(solution)/shard_map/ppermute | solution.py:19
  56.7 2.0 %collective-permute-start.10 = (bf16[32,4096]{1,0:T(8,128)(2,1)S(1)}, bf16[32,4096]{1,0:T(8,128)(2,1)S(1)}, u32[]{:S(2)}, u32[]{:S(2)}) collective-permute-start(bf16[32,4096]{1,0:T(8,128)(2,1)S(1)} %slice.54), channel_id=1, source_target_pairs={{0,224},{32,0},{64,32},{96,64},{128,96},{160,128},{192,160},{224,1... | collective-permute-start | bytes 786440 | tf_op jit(solution)/shard_map/ppermute | solution.py:19
  58.7 0.1 pad_maximum_fusion.1.refs_1_
  58.8 0.3 collective-permute-start.9
  59.1 1.5 fusion.7
  60.7 1.8 %collective-permute-done.10 = bf16[32,4096]{1,0:T(8,128)(2,1)S(1)} collective-permute-done((bf16[32,4096]{1,0:T(8,128)(2,1)S(1)}, bf16[32,4096]{1,0:T(8,128)(2,1)S(1)}, u32[]{:S(2)}, u32[]{:S(2)}) %collective-permute-start.10) | collective-permute-done | bytes 262176 | tf_op jit(solution)/shard_map/ppermute | solution.py:19
  62.4 3.5 %collective-permute-done.9 = bf16[32,4096]{1,0:T(8,128)(2,1)S(1)} collective-permute-done((bf16[32,4096]{1,0:T(8,128)(2,1)S(1)}, bf16[32,4096]{1,0:T(8,128)(2,1)S(1)}, u32[]{:S(2)}, u32[]{:S(2)}) %collective-permute-start.9) | collective-permute-done | bytes 262176 | tf_op jit(solution)/shard_map/ppermute | solution.py:19
  66.0 1.4 fusion.8
  67.4 0.1 pad_maximum_fusion.2.logits_ref
  67.5 0.4 stats.1
  67.9 0.1 broadcast_select_fusion
  68.0 0.7 broadcast_in_dim.61
  68.7 10.7 %all-to-all-start = ((f32[32,3,512]{2,1,0:T(4,128)}), f32[32,3,512]{2,1,0:T(4,128)S(1)}, u32[]{:S(2)}, u32[]{:S(2)}) async-start(f32[32,3,512]{2,1,0:T(4,128)} %bitcast.33), calls=%async_computation | async-start | bytes 524288 | tf_op jit(solution)/shard_map/all_to_all | solution.py:242
  79.4 0.0 reduce-scatter.2.cloned.1.call-start
  79.5 0.0 all-gather.2.cloned.1.call-done.cots_hbm
  79.5 9.2 %lookup.1.looked_hbm = bf16[512,4096]{1,0:T(8,128)(2,1)} custom-call(s32[512,1]{1,0:T(8,128)} %add.133.names_ref, bf16[1024,4224]{1,0:T(8,128)(2,1)} %all-gather.2.cloned.1.call-done.cots_hbm), custom_call_target="tpu_custom_call" | custom-call | flops 4294967296 | bytes 12582912 | tf_op jit(solution)/shard_map/lookup/pallas_call | solution.py:246
  88.8 0.1 slice_reduce_fusion
  88.9 0.1 copy.22
  89.0 0.6 pad_maximum_fusion.6.tokens_ref
  89.6 8.4 %head.1 = (bf16[512,4096]{1,0:T(8,128)(2,1)}, bf16[512,512]{1,0:T(8,128)(2,1)}) custom-call(s32[8]{0:T(128)} %broadcast_multiply_fusion.starts, f32[512,512]{1,0:T(8,128)} %copy-done, s32[512,1]{1,0:T(8,128)} %copy-done.1, f32[3,512]{1,0:T(4,128)} %pad_maximum_fusion.6.tokens_ref, s32[1,512]{1,0:T(1,128)} %bitcast.32, bf16[256,4096]{1,0:T(8,128)(2,1)} %own_hbm.1, ...), custom_call_target="tpu_custom_call" | custom-call | flops 2147483648 | bytes 12582912 | tf_op jit(solution)/shard_map/head/pallas_call | solution.py:268
  98.0 0.0 reduce-scatter.2.cloned.1.call-update
  98.1 1.0 copy-done.5
  99.1 1.6 copy-done.3
  100.7 6.2 %state_terms.1 = (bf16[4,256,1024]{2,1,0:T(8,128)(2,1)S(1)}, bf16[4,256,1024]{2,1,0:T(8,128)(2,1)S(1)}) custom-call(s32[16]{0:T(128)S(1)} %broadcast_select_fusion.1.order, bf16[512,512]{1,0:T(8,128)(2,1)S(1)} %copy-done.5, bf16[256,4096]{1,0:T(8,128)(2,1)S(1)} %copy-done.3, bf16[192,4096]{1,0:T(8,128)(2,1)S(1)} %pad_maximum_fusion.1.refs_1_, ...), custom_call_target="tpu_custom_call" | custom-call | flops 2147483648 | bytes 8388608 | tf_op jit(solution)/shard_map/state_terms/pallas_call | solution.py:297
  106.9 0.3 collective-permute-start.11
  107.2 3.9 %collective-permute-done.11 = bf16[4,256,1024]{2,1,0:T(8,128)(2,1)S(1)} collective-permute-done((bf16[4,256,1024]{2,1,0:T(8,128)(2,1)S(1)}, bf16[4,256,1024]{2,1,0:T(8,128)(2,1)S(1)}, u32[]{:S(2)}, u32[]{:S(2)}) %collective-permute-start.11) | collective-permute-done | bytes 2097184 | tf_op jit(solution)/shard_map/ppermute | solution.py:23
  111.1 1.0 add_convert_fusion
  112.1 19.3 %all_to_all.15 = bf16[4,256,1024]{2,1,0:T(8,128)(2,1)S(1)} all-to-all(bf16[4,256,1024]{2,1,0:T(8,128)(2,1)S(1)} %add_convert_fusion), channel_id=1, replica_groups={{0,4,8,12},{1,5,9,13},{2,6,10,14},{3,7,11,15},{16,17,18,19},{20,21,22,2..., dimensions={0} | all-to-all | bytes 4194304 | tf_op jit(solution)/shard_map/all_to_all | solution.py:40
  131.4 0.4 reduce.3
  131.9 0.9 pad_maximum_fusion.4
  132.7 4.0 %all-to-all-start.2 = ((bf16[4,256,256]{2,1,0:T(8,128)(2,1)}), bf16[4,256,256]{2,1,0:T(8,128)(2,1)S(1)}, u32[]{:S(2)}, u32[]{:S(2)}) async-start(bf16[4,256,256]{2,1,0:T(8,128)(2,1)} %pad_maximum_fusion.4), calls=%async_computation.2 | async-start | bytes 1048576 | tf_op jit(solution)/shard_map/all_to_all | solution.py:40
  136.7 0.6 slice.52
  137.3 6.4 %all-to-all-done.2 = bf16[4,256,256]{2,1,0:T(8,128)(2,1)S(1)} async-done(((bf16[4,256,256]{2,1,0:T(8,128)(2,1)}), bf16[4,256,256]{2,1,0:T(8,128)(2,1)S(1)}, u32[]{:S(2)}, u32[]{:S(2)}) %all-to-all-start.2) | async-done | bytes 524320 | tf_op jit(solution)/shard_map/all_to_all | solution.py:40
  143.6 0.7 reduce_sum.41
  144.4 6.6 %reduce-scatter.2.cloned.1.call-done = bf16[64,4096]{1,0:T(8,128)(2,1)} async-done(((bf16[512,4096]{1,0:T(8,128)(2,1)}), bf16[64,4096]{1,0:T(8,128)(2,1)}) %reduce-scatter.2.cloned.1.call-update) | async-done | bytes 524304 | tf_op jit(solution)/shard_map/reduce_scatter | solution.py:292
  151.0 2.1 %convert_element_type.22 = f32[64,4096]{1,0:T(8,128)} convert(bf16[64,4096]{1,0:T(8,128)(2,1)} %reduce-scatter.2.cloned.1.call-done) | non-fusion elementwise | flops 262144 | bytes 1572864 | tf_op jit(solution)/shard_map/convert_element_type | solution.py:292
  (36 shorter events, 0.3 us)
Async XLA Ops:
  7.2 14.1 %copy-start.9 = (s32[256]{0:T(256)S(1)}, s32[256]{0:T(256)}, u32[]{:S(2)}) copy-start(s32[256]{0:T(256)} %param.11) | copy-start | bytes 3076
  7.2 14.1 %copy-start.10 = (f32[256]{0:T(256)S(1)}, f32[256]{0:T(256)}, u32[]{:S(2)}) copy-start(f32[256]{0:T(256)} %param.12) | copy-start | bytes 3076
  7.2 72.3 %all-gather.2.cloned.1.call-start = ((), (), s32[]{:S(2)}) async-start(), calls=%async_computation.4 | async-start | bytes 8921088 | tf_op jit(solution)/shard_map/all_gather | solution.py:198
  9.1 21.9 %collective-permute-start.2 = (bf16[256,4096]{1,0:T(8,128)(2,1)}, bf16[256,4096]{1,0:T(8,128)(2,1)S(1)}, u32[]{:S(2)}, u32[]{:S(2)}) collective-permute-start(bf16[256,4096]{1,0:T(8,128)(2,1)} %own_hbm.1), channel_id=1, source_target_pairs={{0,16},{16,0},{1,17},{17,1},{2,18},{18,2},{3,19},{19,3},{4,20},{20... | collective-permute-start | bytes 6291464 | tf_op jit(solution)/shard_map/ppermute | solution.py:23
  12.4 15.4 %collective-permute-start = (bf16[64,4096]{1,0:T(8,128)(2,1)}, bf16[64,4096]{1,0:T(8,128)(2,1)}, u32[]{:S(2)}, u32[]{:S(2)}) collective-permute-start(bf16[64,4096]{1,0:T(8,128)(2,1)} %param.10), channel_id=1, source_target_pairs={{0,224},{32,0},{64,32},{96,64},{128,96},{160,128},{192,160},{224,1... | collective-permute-start | bytes 1572872 | tf_op jit(solution)/shard_map/ppermute | solution.py:19
  16.2 14.7 %collective-permute-start.1 = (bf16[64,4096]{1,0:T(8,128)(2,1)}, bf16[64,4096]{1,0:T(8,128)(2,1)}, u32[]{:S(2)}, u32[]{:S(2)}) collective-permute-start(bf16[64,4096]{1,0:T(8,128)(2,1)} %param.10), channel_id=1, source_target_pairs={{0,32},{32,64},{64,96},{96,128},{128,160},{160,192},{192,224},{224... | collective-permute-start | bytes 1572872 | tf_op jit(solution)/shard_map/ppermute | solution.py:19
  16.2 5.0 %collective-permute-start.3 = (s32[256]{0:T(256)}, s32[256]{0:T(256)S(1)}, u32[]{:S(2)}, u32[]{:S(2)}) collective-permute-start(s32[256]{0:T(256)} %param.11), channel_id=1, source_target_pairs={{0,16},{16,0},{1,17},{17,1},{2,18},{18,2},{3,19},{19,3},{4,20},{20... | collective-permute-start | bytes 3080 | tf_op jit(solution)/shard_map/ppermute | solution.py:23
  16.6 4.7 %collective-permute-start.4 = (f32[256]{0:T(256)}, f32[256]{0:T(256)S(1)}, u32[]{:S(2)}, u32[]{:S(2)}) collective-permute-start(f32[256]{0:T(256)} %param.12), channel_id=1, source_target_pairs={{0,16},{16,0},{1,17},{17,1},{2,18},{18,2},{3,19},{19,3},{4,20},{20... | collective-permute-start | bytes 3080 | tf_op jit(solution)/shard_map/ppermute | solution.py:23
  20.7 25.8 %copy-start.8 = (bf16[64,4096]{1,0:T(8,128)(2,1)S(1)}, bf16[64,4096]{1,0:T(8,128)(2,1)}, u32[]{:S(2)}) copy-start(bf16[64,4096]{1,0:T(8,128)(2,1)} %param.10) | copy-start | bytes 1572868
  21.3 46.2 %copy-start.4 = (s32[512]{0:T(512)}, s32[512]{0:T(512)S(1)}, u32[]{:S(2)}) copy-start(s32[512]{0:T(512)S(1)} %pad_add_fusion) | copy-start | bytes 6148
  30.9 17.2 %copy-start.7 = (bf16[256,4096]{1,0:T(8,128)(2,1)}, bf16[256,4096]{1,0:T(8,128)(2,1)S(1)}, u32[]{:S(2)}) copy-start(bf16[256,4096]{1,0:T(8,128)(2,1)S(1)} %collective-permute-done.2.other_hbm) | copy-start | bytes 6291460
  30.9 12.5 %collective-permute-start.5 = (bf16[64,4096]{1,0:T(8,128)(2,1)}, bf16[64,4096]{1,0:T(8,128)(2,1)}, u32[]{:S(2)}, u32[]{:S(2)}) collective-permute-start(bf16[64,4096]{1,0:T(8,128)(2,1)} %collective-permute-done), channel_id=1, source_target_pairs={{0,224},{32,0},{64,32},{96,64},{128,96},{160,128},{192,160},{224,1... | collective-permute-start | bytes 1572872 | tf_op jit(solution)/shard_map/ppermute | solution.py:19
  31.3 13.7 %collective-permute-start.6 = (bf16[64,4096]{1,0:T(8,128)(2,1)}, bf16[64,4096]{1,0:T(8,128)(2,1)S(1)}, u32[]{:S(2)}, u32[]{:S(2)}) collective-permute-start(bf16[64,4096]{1,0:T(8,128)(2,1)} %collective-permute-done.1), channel_id=1, source_target_pairs={{0,32},{32,64},{64,96},{96,128},{128,160},{160,192},{192,224},{224... | collective-permute-start | bytes 1572872 | tf_op jit(solution)/shard_map/ppermute | solution.py:19
  32.6 34.9 %copy-start.1 = (s32[512,1]{1,0:T(8,128)}, s32[512,1]{1,0:T(8,128)S(1)}, u32[]{:S(2)}) copy-start(s32[512,1]{1,0:T(8,128)S(1)} %add.134.names_ref) | copy-start | bytes 6148
  35.0 13.1 %copy-start.6 = (bf16[512,4096]{1,0:T(8,128)(2,1)S(1)}, bf16[512,4096]{1,0:T(8,128)(2,1)}, u32[]{:S(2)}) copy-start(bf16[512,4096]{1,0:T(8,128)(2,1)} %constant_dynamic-update-slice_fusion) | copy-start | bytes 12582916
  45.0 11.7 %collective-permute-start.7 = (bf16[64,4096]{1,0:T(8,128)(2,1)}, bf16[64,4096]{1,0:T(8,128)(2,1)S(1)}, u32[]{:S(2)}, u32[]{:S(2)}) collective-permute-start(bf16[64,4096]{1,0:T(8,128)(2,1)} %collective-permute-done.5), channel_id=1, source_target_pairs={{0,224},{32,0},{64,32},{96,64},{128,96},{160,128},{192,160},{224,1... | collective-permute-start | bytes 1572872 | tf_op jit(solution)/shard_map/ppermute | solution.py:19
  45.4 13.3 %collective-permute-start.8 = (bf16[64,4096]{1,0:T(8,128)(2,1)S(1)}, bf16[64,4096]{1,0:T(8,128)(2,1)S(1)}, u32[]{:S(2)}, u32[]{:S(2)}) collective-permute-start(bf16[64,4096]{1,0:T(8,128)(2,1)S(1)} %collective-permute-done.6), channel_id=1, source_target_pairs={{0,32},{32,64},{64,96},{96,128},{128,160},{160,192},{192,224},{224... | collective-permute-start | bytes 1572872 | tf_op jit(solution)/shard_map/ppermute | solution.py:19
  48.1 1.3 copy-start.2
  56.7 5.7 %collective-permute-start.10 = (bf16[32,4096]{1,0:T(8,128)(2,1)S(1)}, bf16[32,4096]{1,0:T(8,128)(2,1)S(1)}, u32[]{:S(2)}, u32[]{:S(2)}) collective-permute-start(bf16[32,4096]{1,0:T(8,128)(2,1)S(1)} %slice.54), channel_id=1, source_target_pairs={{0,224},{32,0},{64,32},{96,64},{128,96},{160,128},{192,160},{224,1... | collective-permute-start | bytes 786440 | tf_op jit(solution)/shard_map/ppermute | solution.py:19
  58.8 7.1 %collective-permute-start.9 = (bf16[32,4096]{1,0:T(8,128)(2,1)S(1)}, bf16[32,4096]{1,0:T(8,128)(2,1)S(1)}, u32[]{:S(2)}, u32[]{:S(2)}) collective-permute-start(bf16[32,4096]{1,0:T(8,128)(2,1)S(1)} %slice.53), channel_id=1, source_target_pairs={{0,32},{32,64},{64,96},{96,128},{128,160},{160,192},{192,224},{224... | collective-permute-start | bytes 786440 | tf_op jit(solution)/shard_map/ppermute | solution.py:19
  67.5 21.3 %copy-start = (f32[512,512]{1,0:T(8,128)}, f32[512,512]{1,0:T(8,128)S(1)}, u32[]{:S(2)}) copy-start(f32[512,512]{1,0:T(8,128)S(1)} %pad_maximum_fusion.2.logits_ref) | copy-start | bytes 3145732
  68.7 20.1 %all-to-all-start = ((f32[32,3,512]{2,1,0:T(4,128)}), f32[32,3,512]{2,1,0:T(4,128)S(1)}, u32[]{:S(2)}, u32[]{:S(2)}) async-start(f32[32,3,512]{2,1,0:T(4,128)} %bitcast.33), calls=%async_computation | async-start | bytes 524288 | tf_op jit(solution)/shard_map/all_to_all | solution.py:242
  79.4 71.5 %reduce-scatter.2.cloned.1.call-start = ((), (), s32[]{:S(2)}) async-start(), calls=%async_computation.5 | async-start | bytes 4718592 | tf_op jit(solution)/shard_map/reduce_scatter | solution.py:292
  98.0 1.0 copy-start.5
  99.1 1.6 copy-start.3
  106.9 4.2 %collective-permute-start.11 = (bf16[4,256,1024]{2,1,0:T(8,128)(2,1)S(1)}, bf16[4,256,1024]{2,1,0:T(8,128)(2,1)S(1)}, u32[]{:S(2)}, u32[]{:S(2)}) collective-permute-start(bf16[4,256,1024]{2,1,0:T(8,128)(2,1)S(1)} %get-tuple-element.21), channel_id=1, source_target_pairs={{0,16},{16,0},{1,17},{17,1},{2,18},{18,2},{3,19},{19,3},{4,20},{20... | collective-permute-start | bytes 6291464 | tf_op jit(solution)/shard_map/ppermute | solution.py:23
  132.7 10.9 %all-to-all-start.2 = ((bf16[4,256,256]{2,1,0:T(8,128)(2,1)}), bf16[4,256,256]{2,1,0:T(8,128)(2,1)S(1)}, u32[]{:S(2)}, u32[]{:S(2)}) async-start(bf16[4,256,256]{2,1,0:T(8,128)(2,1)} %pad_maximum_fusion.4), calls=%async_computation.2 | async-start | bytes 1048576 | tf_op jit(solution)/shard_map/all_to_all | solution.py:40
Sparse Core Ops, SparseCore 0:
  10.6 62.7 all-gather.1
  98.2 52.7 reduce-scatter.1

commit v4 on v3

--- a/solution.py
+++ b/solution.py
@@ -58,13 +58,19 @@
         out_ref[i * n : (i + 1) * n, depth:] = tail.astype(f32).astype(bf16)
 
 
-def stats_body(logits_ref, names_ref, wanted_ref, out_ref):
+def stats_body(core, logits_ref, names_ref, wanted_ref, out_ref):
     logits = logits_ref[...]
     top = jnp.max(logits, axis=0, keepdims=True)
-    out_ref[0:1] = top
-    out_ref[1:2] = jnp.sum(jnp.exp(logits - top), axis=0, keepdims=True)
+    total = jnp.sum(jnp.exp(logits - top), axis=0, keepdims=True)
     hit = names_ref[...] == wanted_ref[...]
-    out_ref[2:3] = jnp.sum(jnp.where(hit, logits, 0.0), axis=0, keepdims=True)
+    target = jnp.sum(jnp.where(hit, logits, 0.0), axis=0, keepdims=True)
+    peers, tokens = out_ref.shape[0] // 2, out_ref.shape[2] // 2
+    for i, value in enumerate((top, total, target)):
+        turned = jnp.concatenate([value[:, tokens:], value[:, :tokens]], 1)
+        for c in range(2):
+            message = jnp.where(core[0] == c, value, turned)
+            for j in range(peers):
+                out_ref[c * peers + j, i : i + 1] = message
 
 
 def columns(ref, i):
@@ -231,17 +237,14 @@
 
     stats = pl.pallas_call(
         stats_body,
-        out_shape=jax.ShapeDtypeStruct((3, 2 * tokens), f32),
+        out_shape=jax.ShapeDtypeStruct((peers, 3, 2 * tokens), f32),
+        in_specs=[SMEM] + [VMEM] * 3,
+        out_specs=VMEM,
         compiler_params=PARAMS,
         cost_estimate=cost(8 * vocab * tokens, 8 * vocab * tokens),
         name="stats",
-    )(logits, names, wanted)
-    turned = jnp.concatenate([stats[:, tokens:], stats[:, :tokens]], 1)
-    stats = jnp.where(jnp.arange(2)[:, None, None] == c, stats[None], turned[None])
-    stats = jnp.broadcast_to(stats[:, None], (2, NX * NY) + stats.shape[1:])
-    stats = lax.all_to_all(
-        stats.reshape((peers,) + stats.shape[2:]), ("c", "x", "y"), 0, 0, tiled=True
-    )
+    )(c.astype(i32)[None], logits, names, wanted)
+    stats = lax.all_to_all(stats, ("c", "x", "y"), 0, 0, tiled=True)
 
     looked_up = pl.pallas_call(
         lookup_body,

time: 160 us -> 160 us (level)
  local copies, waits for them, and re-layouts: 9.84 us -> 11.5 us
    concatenate x1, local copies, waits for them, and re-layouts: 1.49 us -> 3.17 us  [shards(): states = jnp.concatenate([hidden, other], 0)]
where the time goes in v4:
time: 160 us; the launch traced here: 159 us
  waiting for transfers between devices  48.2 us (30%)
  starting transfers between devices  27.9 us (17%)
  Pallas kernels  26 us (16%)
  blocking collectives  19.3 us (12%)
  between operations  14.3 us (9%)
  local copies, waits for them, and re-layouts  11.5 us (7%)
  other arithmetic  7.6 us (5%)
  matrix products  4.23 us (3%)
    ppermute x8, waiting for transfers between devices, shift(): return lax.ppermute(x, 'z', [(i, (i + k) % NZ) for i in range(NZ)])  31.3 us
    all_to_all x1, blocking collectives, exchange(): lax.all_to_all(x, ('c', 'x', 'y'), 0, 0, axis_index_groups=legs(leg), til...  19.3 us
    all_to_all x1, starting transfers between devices, shards(): stats = lax.all_to_all(stats, ('c', 'x', 'y'), 0, 0, tiled=True)  10.7 us
    pallas_call x1, Pallas kernels, shards(): pl.pallas_call(lookup_body, out_shape=jax.ShapeDtypeStruct((vocab, depth)...  9.24 us
    ppermute x8, starting transfers between devices, shift(): return lax.ppermute(x, 'z', [(i, (i + k) % NZ) for i in range(NZ)])  8.95 us
    pallas_call x1, Pallas kernels, shards(): pl.pallas_call(head_body, out_shape=(jax.ShapeDtypeStruct((vocab, depth),...  8.34 us
    reduce_scatter x1, waiting for transfers between devices, shards(): lax.psum_scatter(head, 'z', scatter_dimension=0, tiled=True).astype(f32)  6.58 us
    unnamed x23, local copies, waits for them, and re-layouts  6.51 us
  transfers between devices with their start and end apart: 16, of which 10 were waited for; matrix products, arithmetic and copies ran while one was open for 11% of the time, Pallas kernels for 10%

profile of v4, /device:TPU:1, one launch (start us, length us, event | category | flops | bytes accessed | tf_op | source)
XLA Modules:
  0.0 159.0 jit_solution(14586979015512328372)
XLA Ops:
  7.2 0.0 copy-start.9
  7.2 0.0 copy-start.10
  7.2 0.0 all-gather.2.cloned.1.call-start
  7.2 1.8 %id_rows.1 = bf16[32,4224]{1,0:T(8,128)(2,1)} custom-call(s32[1,16]{1,0:T(1,128)} %bitcast.36, s32[1,16]{1,0:T(1,128)} %bitcast.37, bf16[16,4096]{1,0:T(8,128)(2,1)} %enc_ref.1, bf16[16,4096]{1,0:T(8,128)(2,1)} %dec_ref.1), custom_call_target="tpu_custom_call" | custom-call | tf_op jit(solution)/shard_map/id_rows/pallas_call | solution.py:198
  9.0 0.0 all-gather.2.cloned.1.call-update
  9.1 3.3 %collective-permute-start.2 = (bf16[256,4096]{1,0:T(8,128)(2,1)}, bf16[256,4096]{1,0:T(8,128)(2,1)}, u32[]{:S(2)}, u32[]{:S(2)}) collective-permute-start(bf16[256,4096]{1,0:T(8,128)(2,1)} %own_hbm.1), channel_id=1, source_target_pairs={{0,16},{16,0},{1,17},{17,1},{2,18},{18,2},{3,19},{19,3},{4,20},{20... | collective-permute-start | bytes 6291464 | tf_op jit(solution)/shard_map/ppermute | solution.py:23
  12.4 3.9 %collective-permute-start = (bf16[64,4096]{1,0:T(8,128)(2,1)}, bf16[64,4096]{1,0:T(8,128)(2,1)S(1)}, u32[]{:S(2)}, u32[]{:S(2)}) collective-permute-start(bf16[64,4096]{1,0:T(8,128)(2,1)} %param.10), channel_id=1, source_target_pairs={{0,224},{32,0},{64,32},{96,64},{128,96},{160,128},{192,160},{224,1... | collective-permute-start | bytes 1572872 | tf_op jit(solution)/shard_map/ppermute | solution.py:19
  16.3 0.4 collective-permute-start.3
  16.6 0.2 collective-permute-start.4
  16.8 0.7 multiply_add_fusion.1
  17.4 0.1 iota_add_fusion.1
  17.5 3.2 %constant_dynamic-update-slice_fusion.1 = bf16[512,4096]{1,0:T(8,128)(2,1)} fusion(bf16[256,4096]{1,0:T(8,128)(2,1)} %own_hbm.1), kind=kLoop, calls=%fused_computation.18 | loop fusion | bytes 4194304
  20.7 0.1 iota_add_fusion
  20.8 7.0 %collective-permute-done = bf16[64,4096]{1,0:T(8,128)(2,1)S(1)} collective-permute-done((bf16[64,4096]{1,0:T(8,128)(2,1)}, bf16[64,4096]{1,0:T(8,128)(2,1)S(1)}, u32[]{:S(2)}, u32[]{:S(2)}) %collective-permute-start) | collective-permute-done | bytes 524320 | tf_op jit(solution)/shard_map/ppermute | solution.py:19
  27.8 3.0 %collective-permute-done.1 = bf16[64,4096]{1,0:T(8,128)(2,1)S(1)} collective-permute-done((bf16[64,4096]{1,0:T(8,128)(2,1)}, bf16[64,4096]{1,0:T(8,128)(2,1)S(1)}, u32[]{:S(2)}, u32[]{:S(2)}) %collective-permute-start.1) | collective-permute-done | bytes 524320 | tf_op jit(solution)/shard_map/ppermute | solution.py:19
  30.8 0.3 collective-permute-start.5
  31.1 1.1 collective-permute-start.6
  32.3 0.5 broadcast_multiply_fusion.starts
  32.8 0.2 add.134.names_ref
  33.0 0.9 add.133.names_ref
  33.9 3.2 %constant_dynamic-update-slice_fusion = bf16[512,4096]{1,0:T(8,128)(2,1)} fusion(bf16[512,4096]{1,0:T(8,128)(2,1)} %constant_dynamic-update-slice_fusion.1, bf16[256,4096]{1,0:T(8,128)(2,1)} %collective-permute-done.2.other_hbm), kind=kLoop, calls=%fused_computation.17 | loop fusion | bytes 4194304 | tf_op jit(solution)/shard_map/concatenate | solution.py:224
  37.1 5.9 %collective-permute-done.5 = bf16[64,4096]{1,0:T(8,128)(2,1)S(1)} collective-permute-done((bf16[64,4096]{1,0:T(8,128)(2,1)S(1)}, bf16[64,4096]{1,0:T(8,128)(2,1)S(1)}, u32[]{:S(2)}, u32[]{:S(2)}) %collective-permute-start.5) | collective-permute-done | bytes 524320 | tf_op jit(solution)/shard_map/ppermute | solution.py:19
  43.1 1.6 collective-permute-done.6
  44.6 0.3 collective-permute-start.7
  44.9 1.2 collective-permute-start.8
  46.1 0.1 pad_maximum_fusion.refs_0_
  46.3 1.3 fusion.5
  47.5 0.0 copy-done.2
  47.6 8.5 %collective-permute-done.7 = bf16[64,4096]{1,0:T(8,128)(2,1)S(1)} collective-permute-done((bf16[64,4096]{1,0:T(8,128)(2,1)S(1)}, bf16[64,4096]{1,0:T(8,128)(2,1)S(1)}, u32[]{:S(2)}, u32[]{:S(2)}) %collective-permute-start.7) | collective-permute-done | bytes 524320 | tf_op jit(solution)/shard_map/ppermute | solution.py:19
  56.1 1.9 %collective-permute-start.10 = (bf16[32,4096]{1,0:T(8,128)(2,1)S(1)}, bf16[32,4096]{1,0:T(8,128)(2,1)S(1)}, u32[]{:S(2)}, u32[]{:S(2)}) collective-permute-start(bf16[32,4096]{1,0:T(8,128)(2,1)S(1)} %slice.46), channel_id=1, source_target_pairs={{0,224},{32,0},{64,32},{96,64},{128,96},{160,128},{192,160},{224,1... | collective-permute-start | bytes 786440 | tf_op jit(solution)/shard_map/ppermute | solution.py:19
  58.0 0.1 pad_maximum_fusion.1.refs_1_
  58.1 0.3 collective-permute-start.9
  58.4 1.5 fusion.6
  59.9 1.9 %collective-permute-done.10 = bf16[32,4096]{1,0:T(8,128)(2,1)S(1)} collective-permute-done((bf16[32,4096]{1,0:T(8,128)(2,1)S(1)}, bf16[32,4096]{1,0:T(8,128)(2,1)S(1)}, u32[]{:S(2)}, u32[]{:S(2)}) %collective-permute-start.10) | collective-permute-done | bytes 262176 | tf_op jit(solution)/shard_map/ppermute | solution.py:19
  61.8 3.4 %collective-permute-done.9 = bf16[32,4096]{1,0:T(8,128)(2,1)S(1)} collective-permute-done((bf16[32,4096]{1,0:T(8,128)(2,1)S(1)}, bf16[32,4096]{1,0:T(8,128)(2,1)S(1)}, u32[]{:S(2)}, u32[]{:S(2)}) %collective-permute-start.9) | collective-permute-done | bytes 262176 | tf_op jit(solution)/shard_map/ppermute | solution.py:19
  65.3 1.4 fusion.7
  66.7 0.1 pad_maximum_fusion.2.logits_ref
  66.8 0.0 copy-start
  66.8 0.4 stats.1
  67.2 0.7 copy-done.4
  67.9 10.7 %all-to-all-start = ((f32[32,3,512]{2,1,0:T(4,128)}), f32[32,3,512]{2,1,0:T(4,128)S(1)}, u32[]{:S(2)}, u32[]{:S(2)}) async-start(f32[32,3,512]{2,1,0:T(4,128)} %copy-done.4), calls=%async_computation | async-start | bytes 524288 | tf_op jit(solution)/shard_map/all_to_all | solution.py:247
  78.6 0.0 reduce-scatter.2.cloned.1.call-start
  78.7 0.0 all-gather.2.cloned.1.call-done.cots_hbm
  78.7 9.2 %lookup.1.looked_hbm = bf16[512,4096]{1,0:T(8,128)(2,1)} custom-call(s32[512,1]{1,0:T(8,128)} %add.133.names_ref, bf16[1024,4224]{1,0:T(8,128)(2,1)} %all-gather.2.cloned.1.call-done.cots_hbm), custom_call_target="tpu_custom_call" | custom-call | flops 4294967296 | bytes 12582912 | tf_op jit(solution)/shard_map/lookup/pallas_call | solution.py:249
  88.0 0.1 slice_reduce_fusion
  88.1 0.1 copy.19
  88.2 0.6 pad_maximum_fusion.5.tokens_ref
  88.8 8.3 %head.1 = (bf16[512,4096]{1,0:T(8,128)(2,1)}, bf16[512,512]{1,0:T(8,128)(2,1)}) custom-call(s32[8]{0:T(128)} %broadcast_multiply_fusion.starts, f32[512,512]{1,0:T(8,128)} %copy-done, s32[512,1]{1,0:T(8,128)} %copy-done.1, f32[3,512]{1,0:T(4,128)} %pad_maximum_fusion.5.tokens_ref, s32[1,512]{1,0:T(1,128)} %bitcast.32, bf16[256,4096]{1,0:T(8,128)(2,1)} %own_hbm.1, ...), custom_call_target="tpu_custom_call" | custom-call | flops 2147483648 | bytes 12582912 | tf_op jit(solution)/shard_map/head/pallas_call | solution.py:271
  97.2 0.0 reduce-scatter.2.cloned.1.call-update
  97.2 1.0 copy-done.6
  98.2 1.6 copy-done.3
  99.8 6.2 %state_terms.1 = (bf16[4,256,1024]{2,1,0:T(8,128)(2,1)S(1)}, bf16[4,256,1024]{2,1,0:T(8,128)(2,1)S(1)}) custom-call(s32[16]{0:T(128)S(1)} %broadcast_select_fusion.order, bf16[512,512]{1,0:T(8,128)(2,1)S(1)} %copy-done.6, bf16[256,4096]{1,0:T(8,128)(2,1)S(1)} %copy-done.3, bf16[192,4096]{1,0:T(8,128)(2,1)S(1)} %pad_maximum_fusion.1.refs_1_, ...), custom_call_target="tpu_custom_call" | custom-call | flops 2147483648 | bytes 8388608 | tf_op jit(solution)/shard_map/state_terms/pallas_call | solution.py:300
  106.0 0.3 collective-permute-start.11
  106.3 3.9 %collective-permute-done.11 = bf16[4,256,1024]{2,1,0:T(8,128)(2,1)S(1)} collective-permute-done((bf16[4,256,1024]{2,1,0:T(8,128)(2,1)S(1)}, bf16[4,256,1024]{2,1,0:T(8,128)(2,1)S(1)}, u32[]{:S(2)}, u32[]{:S(2)}) %collective-permute-start.11) | collective-permute-done | bytes 2097184 | tf_op jit(solution)/shard_map/ppermute | solution.py:23
  110.3 1.0 add_convert_fusion
  111.2 19.3 %all_to_all.15 = bf16[4,256,1024]{2,1,0:T(8,128)(2,1)S(1)} all-to-all(bf16[4,256,1024]{2,1,0:T(8,128)(2,1)S(1)} %add_convert_fusion), channel_id=1, replica_groups={{0,4,8,12},{1,5,9,13},{2,6,10,14},{3,7,11,15},{16,17,18,19},{20,21,22,2..., dimensions={0} | all-to-all | bytes 4194304 | tf_op jit(solution)/shard_map/all_to_all | solution.py:40
  130.5 0.4 reduce.3
  131.0 0.9 pad_maximum_fusion.4
  131.9 4.0 %all-to-all-start.2 = ((bf16[4,256,256]{2,1,0:T(8,128)(2,1)}), bf16[4,256,256]{2,1,0:T(8,128)(2,1)S(1)}, u32[]{:S(2)}, u32[]{:S(2)}) async-start(bf16[4,256,256]{2,1,0:T(8,128)(2,1)} %pad_maximum_fusion.4), calls=%async_computation.2 | async-start | bytes 1048576 | tf_op jit(solution)/shard_map/all_to_all | solution.py:40
  135.9 0.6 slice.44
  136.4 6.4 %all-to-all-done.2 = bf16[4,256,256]{2,1,0:T(8,128)(2,1)S(1)} async-done(((bf16[4,256,256]{2,1,0:T(8,128)(2,1)}), bf16[4,256,256]{2,1,0:T(8,128)(2,1)S(1)}, u32[]{:S(2)}, u32[]{:S(2)}) %all-to-all-start.2) | async-done | bytes 524320 | tf_op jit(solution)/shard_map/all_to_all | solution.py:40
  142.8 0.7 reduce_sum.41
  143.5 6.6 %reduce-scatter.2.cloned.1.call-done = bf16[64,4096]{1,0:T(8,128)(2,1)} async-done(((bf16[512,4096]{1,0:T(8,128)(2,1)}), bf16[64,4096]{1,0:T(8,128)(2,1)}) %reduce-scatter.2.cloned.1.call-update) | async-done | bytes 524304 | tf_op jit(solution)/shard_map/reduce_scatter | solution.py:295
  150.1 2.1 %convert_element_type.22 = f32[64,4096]{1,0:T(8,128)} convert(bf16[64,4096]{1,0:T(8,128)(2,1)} %reduce-scatter.2.cloned.1.call-done) | non-fusion elementwise | flops 262144 | bytes 1572864 | tf_op jit(solution)/shard_map/convert_element_type | solution.py:295
  (32 shorter events, 0.2 us)
Async XLA Ops:
  7.2 13.6 %copy-start.9 = (s32[256]{0:T(256)S(1)}, s32[256]{0:T(256)}, u32[]{:S(2)}) copy-start(s32[256]{0:T(256)} %param.11) | copy-start | bytes 3076
  7.2 13.6 %copy-start.10 = (f32[256]{0:T(256)S(1)}, f32[256]{0:T(256)}, u32[]{:S(2)}) copy-start(f32[256]{0:T(256)} %param.12) | copy-start | bytes 3076
  7.2 71.5 %all-gather.2.cloned.1.call-start = ((), (), s32[]{:S(2)}) async-start(), calls=%async_computation.4 | async-start | bytes 8921088 | tf_op jit(solution)/shard_map/all_gather | solution.py:204
  9.1 21.8 %collective-permute-start.2 = (bf16[256,4096]{1,0:T(8,128)(2,1)}, bf16[256,4096]{1,0:T(8,128)(2,1)}, u32[]{:S(2)}, u32[]{:S(2)}) collective-permute-start(bf16[256,4096]{1,0:T(8,128)(2,1)} %own_hbm.1), channel_id=1, source_target_pairs={{0,16},{16,0},{1,17},{17,1},{2,18},{18,2},{3,19},{19,3},{4,20},{20... | collective-permute-start | bytes 6291464 | tf_op jit(solution)/shard_map/ppermute | solution.py:23
  12.4 15.4 %collective-permute-start = (bf16[64,4096]{1,0:T(8,128)(2,1)}, bf16[64,4096]{1,0:T(8,128)(2,1)S(1)}, u32[]{:S(2)}, u32[]{:S(2)}) collective-permute-start(bf16[64,4096]{1,0:T(8,128)(2,1)} %param.10), channel_id=1, source_target_pairs={{0,224},{32,0},{64,32},{96,64},{128,96},{160,128},{192,160},{224,1... | collective-permute-start | bytes 1572872 | tf_op jit(solution)/shard_map/ppermute | solution.py:19
  16.3 14.6 %collective-permute-start.1 = (bf16[64,4096]{1,0:T(8,128)(2,1)}, bf16[64,4096]{1,0:T(8,128)(2,1)S(1)}, u32[]{:S(2)}, u32[]{:S(2)}) collective-permute-start(bf16[64,4096]{1,0:T(8,128)(2,1)} %param.10), channel_id=1, source_target_pairs={{0,32},{32,64},{64,96},{96,128},{128,160},{160,192},{192,224},{224... | collective-permute-start | bytes 1572872 | tf_op jit(solution)/shard_map/ppermute | solution.py:19
  16.3 4.5 %collective-permute-start.3 = (s32[256]{0:T(256)}, s32[256]{0:T(256)S(1)}, u32[]{:S(2)}, u32[]{:S(2)}) collective-permute-start(s32[256]{0:T(256)} %param.11), channel_id=1, source_target_pairs={{0,16},{16,0},{1,17},{17,1},{2,18},{18,2},{3,19},{19,3},{4,20},{20... | collective-permute-start | bytes 3080 | tf_op jit(solution)/shard_map/ppermute | solution.py:23
  16.6 4.2 %collective-permute-start.4 = (f32[256]{0:T(256)}, f32[256]{0:T(256)S(1)}, u32[]{:S(2)}, u32[]{:S(2)}) collective-permute-start(f32[256]{0:T(256)} %param.12), channel_id=1, source_target_pairs={{0,16},{16,0},{1,17},{17,1},{2,18},{18,2},{3,19},{19,3},{4,20},{20... | collective-permute-start | bytes 3080 | tf_op jit(solution)/shard_map/ppermute | solution.py:23
  20.7 25.4 %copy-start.8 = (bf16[64,4096]{1,0:T(8,128)(2,1)S(1)}, bf16[64,4096]{1,0:T(8,128)(2,1)}, u32[]{:S(2)}) copy-start(bf16[64,4096]{1,0:T(8,128)(2,1)} %param.10) | copy-start | bytes 1572868
  20.8 46.0 %copy-start.5 = (s32[512]{0:T(512)}, s32[512]{0:T(512)S(1)}, u32[]{:S(2)}) copy-start(s32[512]{0:T(512)S(1)} %pad_add_fusion) | copy-start | bytes 6148
  30.8 12.2 %collective-permute-start.5 = (bf16[64,4096]{1,0:T(8,128)(2,1)S(1)}, bf16[64,4096]{1,0:T(8,128)(2,1)S(1)}, u32[]{:S(2)}, u32[]{:S(2)}) collective-permute-start(bf16[64,4096]{1,0:T(8,128)(2,1)S(1)} %collective-permute-done), channel_id=1, source_target_pairs={{0,224},{32,0},{64,32},{96,64},{128,96},{160,128},{192,160},{224,1... | collective-permute-start | bytes 1572872 | tf_op jit(solution)/shard_map/ppermute | solution.py:19
  31.1 13.5 %collective-permute-start.6 = (bf16[64,4096]{1,0:T(8,128)(2,1)S(1)}, bf16[64,4096]{1,0:T(8,128)(2,1)S(1)}, u32[]{:S(2)}, u32[]{:S(2)}) collective-permute-start(bf16[64,4096]{1,0:T(8,128)(2,1)S(1)} %collective-permute-done.1), channel_id=1, source_target_pairs={{0,32},{32,64},{64,96},{96,128},{128,160},{160,192},{192,224},{224... | collective-permute-start | bytes 1572872 | tf_op jit(solution)/shard_map/ppermute | solution.py:19
  33.0 33.7 %copy-start.1 = (s32[512,1]{1,0:T(8,128)}, s32[512,1]{1,0:T(8,128)S(1)}, u32[]{:S(2)}) copy-start(s32[512,1]{1,0:T(8,128)S(1)} %add.134.names_ref) | copy-start | bytes 6148
  37.1 9.1 %copy-start.7 = (bf16[512,4096]{1,0:T(8,128)(2,1)S(1)}, bf16[512,4096]{1,0:T(8,128)(2,1)}, u32[]{:S(2)}) copy-start(bf16[512,4096]{1,0:T(8,128)(2,1)} %constant_dynamic-update-slice_fusion) | copy-start | bytes 12582916
  44.6 11.4 %collective-permute-start.7 = (bf16[64,4096]{1,0:T(8,128)(2,1)S(1)}, bf16[64,4096]{1,0:T(8,128)(2,1)S(1)}, u32[]{:S(2)}, u32[]{:S(2)}) collective-permute-start(bf16[64,4096]{1,0:T(8,128)(2,1)S(1)} %collective-permute-done.5), channel_id=1, source_target_pairs={{0,224},{32,0},{64,32},{96,64},{128,96},{160,128},{192,160},{224,1... | collective-permute-start | bytes 1572872 | tf_op jit(solution)/shard_map/ppermute | solution.py:19
  44.9 13.1 %collective-permute-start.8 = (bf16[64,4096]{1,0:T(8,128)(2,1)S(1)}, bf16[64,4096]{1,0:T(8,128)(2,1)S(1)}, u32[]{:S(2)}, u32[]{:S(2)}) collective-permute-start(bf16[64,4096]{1,0:T(8,128)(2,1)S(1)} %collective-permute-done.6), channel_id=1, source_target_pairs={{0,32},{32,64},{64,96},{96,128},{128,160},{160,192},{192,224},{224... | collective-permute-start | bytes 1572872 | tf_op jit(solution)/shard_map/ppermute | solution.py:19
  46.2 1.3 copy-start.2
  56.1 5.7 %collective-permute-start.10 = (bf16[32,4096]{1,0:T(8,128)(2,1)S(1)}, bf16[32,4096]{1,0:T(8,128)(2,1)S(1)}, u32[]{:S(2)}, u32[]{:S(2)}) collective-permute-start(bf16[32,4096]{1,0:T(8,128)(2,1)S(1)} %slice.46), channel_id=1, source_target_pairs={{0,224},{32,0},{64,32},{96,64},{128,96},{160,128},{192,160},{224,1... | collective-permute-start | bytes 786440 | tf_op jit(solution)/shard_map/ppermute | solution.py:19
  58.1 7.1 %collective-permute-start.9 = (bf16[32,4096]{1,0:T(8,128)(2,1)S(1)}, bf16[32,4096]{1,0:T(8,128)(2,1)S(1)}, u32[]{:S(2)}, u32[]{:S(2)}) collective-permute-start(bf16[32,4096]{1,0:T(8,128)(2,1)S(1)} %slice.45), channel_id=1, source_target_pairs={{0,32},{32,64},{64,96},{96,128},{128,160},{160,192},{192,224},{224... | collective-permute-start | bytes 786440 | tf_op jit(solution)/shard_map/ppermute | solution.py:19
  66.8 21.2 %copy-start = (f32[512,512]{1,0:T(8,128)}, f32[512,512]{1,0:T(8,128)S(1)}, u32[]{:S(2)}) copy-start(f32[512,512]{1,0:T(8,128)S(1)} %pad_maximum_fusion.2.logits_ref) | copy-start | bytes 3145732
  67.2 0.7 copy-start.4
  67.9 20.0 %all-to-all-start = ((f32[32,3,512]{2,1,0:T(4,128)}), f32[32,3,512]{2,1,0:T(4,128)S(1)}, u32[]{:S(2)}, u32[]{:S(2)}) async-start(f32[32,3,512]{2,1,0:T(4,128)} %copy-done.4), calls=%async_computation | async-start | bytes 524288 | tf_op jit(solution)/shard_map/all_to_all | solution.py:247
  78.6 71.5 %reduce-scatter.2.cloned.1.call-start = ((), (), s32[]{:S(2)}) async-start(), calls=%async_computation.5 | async-start | bytes 4718592 | tf_op jit(solution)/shard_map/reduce_scatter | solution.py:295
  97.2 1.0 copy-start.6
  98.2 1.6 %copy-start.3 = (bf16[256,4096]{1,0:T(8,128)(2,1)S(1)}, bf16[256,4096]{1,0:T(8,128)(2,1)}, u32[]{:S(2)}) copy-start(bf16[256,4096]{1,0:T(8,128)(2,1)} %copy-done.2) | copy-start | bytes 6291460
  106.0 4.2 %collective-permute-start.11 = (bf16[4,256,1024]{2,1,0:T(8,128)(2,1)S(1)}, bf16[4,256,1024]{2,1,0:T(8,128)(2,1)S(1)}, u32[]{:S(2)}, u32[]{:S(2)}) collective-permute-start(bf16[4,256,1024]{2,1,0:T(8,128)(2,1)S(1)} %get-tuple-element.21), channel_id=1, source_target_pairs={{0,16},{16,0},{1,17},{17,1},{2,18},{18,2},{3,19},{19,3},{4,20},{20... | collective-permute-start | bytes 6291464 | tf_op jit(solution)/shard_map/ppermute | solution.py:23
  131.9 10.9 %all-to-all-start.2 = ((bf16[4,256,256]{2,1,0:T(8,128)(2,1)}), bf16[4,256,256]{2,1,0:T(8,128)(2,1)S(1)}, u32[]{:S(2)}, u32[]{:S(2)}) async-start(bf16[4,256,256]{2,1,0:T(8,128)(2,1)} %pad_maximum_fusion.4), calls=%async_computation.2 | async-start | bytes 1048576 | tf_op jit(solution)/shard_map/all_to_all | solution.py:40
Sparse Core Ops, SparseCore 0:
  10.6 62.7 all-gather.1
  97.3 52.7 reduce-scatter.1

commit v5 on v4

--- a/solution.py
+++ b/solution.py
@@ -109,7 +109,7 @@
 
 
 def head_body(
-    starts, logits_ref, names_ref, tokens_ref, wanted_ref, own_hbm, other_hbm, looked_hbm,
+    starts, logits_ref, names_ref, stats_ref, scale_ref, wanted_ref, own_hbm, other_hbm, looked_hbm,
     out_hbm, d_ref, sorted_ref, own_ref, other_ref, looked_ref, sums, in_sems, out_sems,
 ):
     steps = out_hbm.shape[1] // WIDTH
@@ -127,9 +127,12 @@
     for i in range(steps):
         for fetch in fetches(i):
             fetch.start()
-    share = jnp.exp(logits_ref[...] - tokens_ref[0:1]) * (1.0 / tokens_ref[1:2])
+    tops = stats_ref[:, 0, :]
+    top = jnp.max(tops, axis=0, keepdims=True)
+    total = jnp.sum(stats_ref[:, 1, :] * jnp.exp(tops - top), axis=0, keepdims=True)
+    share = jnp.exp(logits_ref[...] - top) * (1.0 / total)
     hit = (names_ref[...] == wanted_ref[...]).astype(f32)
-    d_ref[...] = (tokens_ref[2:3] * (share - hit)).astype(bf16)
+    d_ref[...] = (scale_ref[...] * (share - hit)).astype(bf16)
     pieces = starts.shape[0]
     rows = d_ref.shape[0] // pieces
     for k in range(pieces):
@@ -274,7 +277,7 @@
             jax.ShapeDtypeStruct((vocab, depth), bf16),
             jax.ShapeDtypeStruct((vocab, 2 * tokens), bf16),
         ),
-        in_specs=[SMEM] + [VMEM] * 4 + [ANY] * 3,
+        in_specs=[SMEM] + [VMEM] * 5 + [ANY] * 3,
         out_specs=(ANY, VMEM),
         scratch_shapes=[
             pltpu.VMEM((vocab, 2 * tokens), bf16),
@@ -289,7 +292,7 @@
         cost_estimate=cost(4 * vocab * tokens * depth, 4 * vocab * depth + 4 * tokens * depth),
         name="head",
     )(
-        places * rows, logits, names, jnp.concatenate([row_max[None], row_sum[None], scales]),
+        places * rows, logits, names, stats, scales,
         wanted, hidden, other, looked_up,
     )
     grad_table = lax.psum_scatter(head, "z", scatter_dimension=0, tiled=True).astype(f32)

time: 160 us -> 160 us (level)
  blocking collectives: 19.3 us -> 0 us
  waiting for transfers between devices: 48.2 us -> 62.2 us
  starting transfers between devices: 27.9 us -> 32 us
  other arithmetic: 7.6 us -> 10.3 us
    all_to_all x1 -> x0, blocking collectives: 19.3 us -> none  [exchange(): lax.all_to_all(x, ('c', 'x', 'y'), 0, 0, axis_index_groups=legs(leg), til...]
    all_to_all x1 -> x2, waiting for transfers between devices: 6.36 us -> 21.7 us  [exchange(): lax.all_to_all(x, ('c', 'x', 'y'), 0, 0, axis_index_groups=legs(leg), til...]
    all_to_all x1 -> x2, starting transfers between devices: 3.99 us -> 7.96 us  [exchange(): lax.all_to_all(x, ('c', 'x', 'y'), 0, 0, axis_index_groups=legs(leg), til...]
    reduce_scatter x1, waiting for transfers between devices: 6.58 us -> 4.91 us  [shards(): lax.psum_scatter(head, 'z', scatter_dimension=0, tiled=True).astype(f32)]
    concatenate x1, local copies, waits for them, and re-layouts: 3.17 us -> 1.51 us  [shards(): states = jnp.concatenate([hidden, other], 0)]
    unnamed x23 -> x29, local copies, waits for them, and re-layouts: 6.51 us -> 7.21 us
  transfers between devices with their start and end apart: 16 -> 17, of which waited for: 10 -> 11; matrix products, arithmetic and copies ran while one was open for 11% -> 12% of each run, Pallas kernels for 10% -> 10%
where the time goes in v5:
time: 160 us
  waiting for transfers between devices  62.2 us (39%)
  starting transfers between devices  32 us (20%)
  Pallas kernels  26 us (16%)
  between operations  14.3 us (9%)
  local copies, waits for them, and re-layouts  10.5 us (7%)
  other arithmetic  10.3 us (6%)
  matrix products  4.2 us (3%)
    ppermute x8, waiting for transfers between devices, shift(): return lax.ppermute(x, 'z', [(i, (i + k) % NZ) for i in range(NZ)])  31.6 us
    all_to_all x2, waiting for transfers between devices, exchange(): lax.all_to_all(x, ('c', 'x', 'y'), 0, 0, axis_index_groups=legs(leg), til...  21.7 us
    all_to_all x1, starting transfers between devices, shards(): stats = lax.all_to_all(stats, ('c', 'x', 'y'), 0, 0, tiled=True)  10.7 us
    pallas_call x1, Pallas kernels, shards(): pl.pallas_call(lookup_body, out_shape=jax.ShapeDtypeStruct((vocab, depth)...  9.26 us
    ppermute x8, starting transfers between devices, shift(): return lax.ppermute(x, 'z', [(i, (i + k) % NZ) for i in range(NZ)])  9.05 us
    pallas_call x1, Pallas kernels, shards(): pl.pallas_call(head_body, out_shape=(jax.ShapeDtypeStruct((vocab, depth),...  8.4 us
    all_to_all x2, starting transfers between devices, exchange(): lax.all_to_all(x, ('c', 'x', 'y'), 0, 0, axis_index_groups=legs(leg), til...  7.96 us
    unnamed x29, local copies, waits for them, and re-layouts  7.21 us
  transfers between devices with their start and end apart: 17, of which 11 were waited for; matrix products, arithmetic and copies ran while one was open for 12% of the time, Pallas kernels for 10%

profile of v5, /device:TPU:1, one launch (start us, length us, event | category | flops | bytes accessed | tf_op | source)
XLA Modules:
  0.0 159.6 jit_solution(10651023066853274415)
XLA Ops:
  7.2 0.0 copy-start.13
  7.2 0.0 all-gather.2.cloned.1.call-start
  7.2 1.8 %id_rows.1 = bf16[32,4224]{1,0:T(8,128)(2,1)} custom-call(s32[1,16]{1,0:T(1,128)} %bitcast.32, s32[1,16]{1,0:T(1,128)} %bitcast.33, bf16[16,4096]{1,0:T(8,128)(2,1)} %enc_ref.1, bf16[16,4096]{1,0:T(8,128)(2,1)} %dec_ref.1), custom_call_target="tpu_custom_call" | custom-call | tf_op jit(solution)/shard_map/id_rows/pallas_call | solution.py:201
  9.0 0.0 all-gather.2.cloned.1.call-update
  9.1 3.3 %collective-permute-start.2 = (bf16[256,4096]{1,0:T(8,128)(2,1)}, bf16[256,4096]{1,0:T(8,128)(2,1)S(1)}, u32[]{:S(2)}, u32[]{:S(2)}) collective-permute-start(bf16[256,4096]{1,0:T(8,128)(2,1)} %own_hbm.1), channel_id=1, source_target_pairs={{0,16},{16,0},{1,17},{17,1},{2,18},{18,2},{3,19},{19,3},{4,20},{20... | collective-permute-start | bytes 6291464 | tf_op jit(solution)/shard_map/ppermute | solution.py:23
  12.4 3.9 %collective-permute-start = (bf16[64,4096]{1,0:T(8,128)(2,1)}, bf16[64,4096]{1,0:T(8,128)(2,1)}, u32[]{:S(2)}, u32[]{:S(2)}) collective-permute-start(bf16[64,4096]{1,0:T(8,128)(2,1)} %param.10), channel_id=1, source_target_pairs={{0,224},{32,0},{64,32},{96,64},{128,96},{160,128},{192,160},{224,1... | collective-permute-start | bytes 1572872 | tf_op jit(solution)/shard_map/ppermute | solution.py:19
  16.2 0.4 collective-permute-start.3
  16.6 0.2 collective-permute-start.4
  16.8 0.7 multiply_add_fusion.1
  17.4 0.1 iota_add_fusion.1
  17.5 3.2 %constant_dynamic-update-slice_fusion.1 = bf16[512,4096]{1,0:T(8,128)(2,1)} fusion(bf16[256,4096]{1,0:T(8,128)(2,1)} %own_hbm.1), kind=kLoop, calls=%fused_computation.17 | loop fusion | bytes 4194304
  20.7 0.1 iota_add_fusion
  20.8 0.6 pad_maximum_fusion.5
  21.4 6.4 %collective-permute-done = bf16[64,4096]{1,0:T(8,128)(2,1)} collective-permute-done((bf16[64,4096]{1,0:T(8,128)(2,1)}, bf16[64,4096]{1,0:T(8,128)(2,1)}, u32[]{:S(2)}, u32[]{:S(2)}) %collective-permute-start) | collective-permute-done | bytes 524320 | tf_op jit(solution)/shard_map/ppermute | solution.py:19
  27.8 3.1 %collective-permute-done.1 = bf16[64,4096]{1,0:T(8,128)(2,1)} collective-permute-done((bf16[64,4096]{1,0:T(8,128)(2,1)}, bf16[64,4096]{1,0:T(8,128)(2,1)}, u32[]{:S(2)}, u32[]{:S(2)}) %collective-permute-start.1) | collective-permute-done | bytes 524320 | tf_op jit(solution)/shard_map/ppermute | solution.py:19
  30.9 0.4 collective-permute-start.5
  31.3 1.1 collective-permute-start.6
  32.4 0.5 broadcast_multiply_fusion.starts
  32.9 0.2 add.134.names_ref
  33.1 0.9 add.133.names_ref
  34.0 1.5 constant_dynamic-update-slice_fusion
  35.5 8.0 %collective-permute-done.5 = bf16[64,4096]{1,0:T(8,128)(2,1)} collective-permute-done((bf16[64,4096]{1,0:T(8,128)(2,1)}, bf16[64,4096]{1,0:T(8,128)(2,1)}, u32[]{:S(2)}, u32[]{:S(2)}) %collective-permute-start.5) | collective-permute-done | bytes 524320 | tf_op jit(solution)/shard_map/ppermute | solution.py:19
  43.5 1.5 collective-permute-done.6
  45.0 0.4 collective-permute-start.7
  45.4 1.1 collective-permute-start.8
  46.5 1.6 pad_maximum_fusion.refs_0_
  48.1 1.3 fusion.6
  49.4 0.0 copy-done.2
  49.4 7.3 %collective-permute-done.7 = bf16[64,4096]{1,0:T(8,128)(2,1)S(1)} collective-permute-done((bf16[64,4096]{1,0:T(8,128)(2,1)}, bf16[64,4096]{1,0:T(8,128)(2,1)S(1)}, u32[]{:S(2)}, u32[]{:S(2)}) %collective-permute-start.7) | collective-permute-done | bytes 524320 | tf_op jit(solution)/shard_map/ppermute | solution.py:19
  56.7 2.0 %collective-permute-start.10 = (bf16[32,4096]{1,0:T(8,128)(2,1)S(1)}, bf16[32,4096]{1,0:T(8,128)(2,1)S(1)}, u32[]{:S(2)}, u32[]{:S(2)}) collective-permute-start(bf16[32,4096]{1,0:T(8,128)(2,1)S(1)} %slice.46), channel_id=1, source_target_pairs={{0,224},{32,0},{64,32},{96,64},{128,96},{160,128},{192,160},{224,1... | collective-permute-start | bytes 786440 | tf_op jit(solution)/shard_map/ppermute | solution.py:19
  58.7 0.1 pad_maximum_fusion.1.refs_1_
  58.9 0.3 collective-permute-start.9
  59.1 1.5 fusion.7
  60.7 1.8 %collective-permute-done.10 = bf16[32,4096]{1,0:T(8,128)(2,1)S(1)} collective-permute-done((bf16[32,4096]{1,0:T(8,128)(2,1)S(1)}, bf16[32,4096]{1,0:T(8,128)(2,1)S(1)}, u32[]{:S(2)}, u32[]{:S(2)}) %collective-permute-start.10) | collective-permute-done | bytes 262176 | tf_op jit(solution)/shard_map/ppermute | solution.py:19
  62.4 3.5 %collective-permute-done.9 = bf16[32,4096]{1,0:T(8,128)(2,1)S(1)} collective-permute-done((bf16[32,4096]{1,0:T(8,128)(2,1)S(1)}, bf16[32,4096]{1,0:T(8,128)(2,1)S(1)}, u32[]{:S(2)}, u32[]{:S(2)}) %collective-permute-start.9) | collective-permute-done | bytes 262176 | tf_op jit(solution)/shard_map/ppermute | solution.py:19
  66.0 1.4 fusion.8
  67.4 0.1 pad_maximum_fusion.2.logits_ref
  67.5 0.4 stats.1
  67.9 0.7 copy-done.4
  68.6 10.7 %all-to-all-start = ((f32[32,3,512]{2,1,0:T(4,128)}), f32[32,3,512]{2,1,0:T(4,128)S(1)}, u32[]{:S(2)}, u32[]{:S(2)}) async-start(f32[32,3,512]{2,1,0:T(4,128)} %copy-done.4), calls=%async_computation | async-start | bytes 524288 | tf_op jit(solution)/shard_map/all_to_all | solution.py:250
  79.3 0.0 reduce-scatter.2.cloned.1.call-start
  79.4 0.0 all-gather.2.cloned.1.call-done.cots_hbm
  79.4 9.3 %lookup.1.looked_hbm = bf16[512,4096]{1,0:T(8,128)(2,1)} custom-call(s32[512,1]{1,0:T(8,128)} %add.133.names_ref, bf16[1024,4224]{1,0:T(8,128)(2,1)} %all-gather.2.cloned.1.call-done.cots_hbm), custom_call_target="tpu_custom_call" | custom-call | flops 4294967296 | bytes 12582912 | tf_op jit(solution)/shard_map/lookup/pallas_call | solution.py:252
  88.7 0.7 copy-done.9
  89.4 8.4 %head.1 = (bf16[512,4096]{1,0:T(8,128)(2,1)}, bf16[512,512]{1,0:T(8,128)(2,1)}) custom-call(s32[8]{0:T(128)} %broadcast_multiply_fusion.starts, f32[512,512]{1,0:T(8,128)} %copy-done, s32[512,1]{1,0:T(8,128)} %copy-done.1, f32[32,3,512]{2,1,0:T(4,128)} %copy-done.9, f32[1,512]{1,0:T(1,128)} %bitcast.31, s32[1,512]{1,0:T(1,128)} %bitcast.30, ...), custom_call_target="tpu_custom_call" | custom-call | flops 2147483648 | bytes 12582912 | tf_op jit(solution)/shard_map/head/pallas_call | solution.py:274
  97.8 0.0 reduce-scatter.2.cloned.1.call-update
  97.8 1.0 copy-done.6
  98.8 1.6 copy-done.3
  100.4 6.2 %state_terms.1 = (bf16[4,256,1024]{2,1,0:T(8,128)(2,1)S(1)}, bf16[4,256,1024]{2,1,0:T(8,128)(2,1)S(1)}) custom-call(s32[16]{0:T(128)S(1)} %broadcast_select_fusion.order, bf16[512,512]{1,0:T(8,128)(2,1)S(1)} %copy-done.6, bf16[256,4096]{1,0:T(8,128)(2,1)S(1)} %copy-done.3, bf16[192,4096]{1,0:T(8,128)(2,1)S(1)} %pad_maximum_fusion.1.refs_1_, ...), custom_call_target="tpu_custom_call" | custom-call | flops 2147483648 | bytes 8388608 | tf_op jit(solution)/shard_map/state_terms/pallas_call | solution.py:303
  106.6 0.3 collective-permute-start.11
  106.9 3.9 %collective-permute-done.11 = bf16[4,256,1024]{2,1,0:T(8,128)(2,1)S(1)} collective-permute-done((bf16[4,256,1024]{2,1,0:T(8,128)(2,1)S(1)}, bf16[4,256,1024]{2,1,0:T(8,128)(2,1)S(1)}, u32[]{:S(2)}, u32[]{:S(2)}) %collective-permute-start.11) | collective-permute-done | bytes 2097184 | tf_op jit(solution)/shard_map/ppermute | solution.py:23
  110.8 2.3 %add_convert_fusion = bf16[4,256,1024]{2,1,0:T(8,128)(2,1)} fusion(bf16[4,256,1024]{2,1,0:T(8,128)(2,1)S(1)} %collective-permute-done.11, bf16[4,256,1024]{2,1,0:T(8,128)(2,1)S(1)} %get-tuple-element.20), kind=kLoop, calls=%fused_computation | loop fusion | flops 4194304 | bytes 6291456 | tf_op jit(solution)/shard_map/convert_element_type | solution.py:315
  113.2 4.3 %all-to-all-start.1 = ((bf16[4,256,1024]{2,1,0:T(8,128)(2,1)}), bf16[4,256,1024]{2,1,0:T(8,128)(2,1)S(1)}, u32[]{:S(2)}, u32[]{:S(2)}) async-start(bf16[4,256,1024]{2,1,0:T(8,128)(2,1)} %add_convert_fusion), calls=%async_computation.1 | async-start | bytes 4194304 | tf_op jit(solution)/shard_map/all_to_all | solution.py:40
  117.4 0.1 copy.20
  117.5 0.1 fusion.5
  117.6 15.5 %all-to-all-done.1 = bf16[4,256,1024]{2,1,0:T(8,128)(2,1)S(1)} async-done(((bf16[4,256,1024]{2,1,0:T(8,128)(2,1)}), bf16[4,256,1024]{2,1,0:T(8,128)(2,1)S(1)}, u32[]{:S(2)}, u32[]{:S(2)}) %all-to-all-start.1) | async-done | bytes 2097184 | tf_op jit(solution)/shard_map/all_to_all | solution.py:40
  133.1 0.4 reduce.3
  133.6 0.9 pad_maximum_fusion.4
  134.4 3.7 %all-to-all-start.2 = ((bf16[4,256,256]{2,1,0:T(8,128)(2,1)}), bf16[4,256,256]{2,1,0:T(8,128)(2,1)S(1)}, u32[]{:S(2)}, u32[]{:S(2)}) async-start(bf16[4,256,256]{2,1,0:T(8,128)(2,1)} %pad_maximum_fusion.4), calls=%async_computation.2 | async-start | bytes 1048576 | tf_op jit(solution)/shard_map/all_to_all | solution.py:40
  138.2 0.6 slice.44
  138.8 6.3 %all-to-all-done.2 = bf16[4,256,256]{2,1,0:T(8,128)(2,1)S(1)} async-done(((bf16[4,256,256]{2,1,0:T(8,128)(2,1)}), bf16[4,256,256]{2,1,0:T(8,128)(2,1)S(1)}, u32[]{:S(2)}, u32[]{:S(2)}) %all-to-all-start.2) | async-done | bytes 524320 | tf_op jit(solution)/shard_map/all_to_all | solution.py:40
  145.0 0.7 reduce_sum.40
  145.8 4.9 %reduce-scatter.2.cloned.1.call-done = bf16[64,4096]{1,0:T(8,128)(2,1)} async-done(((bf16[512,4096]{1,0:T(8,128)(2,1)}), bf16[64,4096]{1,0:T(8,128)(2,1)}) %reduce-scatter.2.cloned.1.call-update) | async-done | bytes 524304 | tf_op jit(solution)/shard_map/reduce_scatter | solution.py:298
  150.7 2.1 %convert_element_type.22 = f32[64,4096]{1,0:T(8,128)} convert(bf16[64,4096]{1,0:T(8,128)(2,1)} %reduce-scatter.2.cloned.1.call-done) | non-fusion elementwise | flops 262144 | bytes 1572864 | tf_op jit(solution)/shard_map/convert_element_type | solution.py:298
  (38 shorter events, 0.3 us)
Async XLA Ops:
  7.2 13.6 %copy-start.12 = (s32[256]{0:T(256)S(1)}, s32[256]{0:T(256)}, u32[]{:S(2)}) copy-start(s32[256]{0:T(256)} %param.11) | copy-start | bytes 3076
  7.2 13.6 %copy-start.13 = (f32[256]{0:T(256)S(1)}, f32[256]{0:T(256)}, u32[]{:S(2)}) copy-start(f32[256]{0:T(256)} %param.12) | copy-start | bytes 3076
  7.2 72.2 %all-gather.2.cloned.1.call-start = ((), (), s32[]{:S(2)}) async-start(), calls=%async_computation.4 | async-start | bytes 8921088 | tf_op jit(solution)/shard_map/all_gather | solution.py:207
  9.1 21.9 %collective-permute-start.2 = (bf16[256,4096]{1,0:T(8,128)(2,1)}, bf16[256,4096]{1,0:T(8,128)(2,1)S(1)}, u32[]{:S(2)}, u32[]{:S(2)}) collective-permute-start(bf16[256,4096]{1,0:T(8,128)(2,1)} %own_hbm.1), channel_id=1, source_target_pairs={{0,16},{16,0},{1,17},{17,1},{2,18},{18,2},{3,19},{19,3},{4,20},{20... | collective-permute-start | bytes 6291464 | tf_op jit(solution)/shard_map/ppermute | solution.py:23
  12.4 15.4 %collective-permute-start = (bf16[64,4096]{1,0:T(8,128)(2,1)}, bf16[64,4096]{1,0:T(8,128)(2,1)}, u32[]{:S(2)}, u32[]{:S(2)}) collective-permute-start(bf16[64,4096]{1,0:T(8,128)(2,1)} %param.10), channel_id=1, source_target_pairs={{0,224},{32,0},{64,32},{96,64},{128,96},{160,128},{192,160},{224,1... | collective-permute-start | bytes 1572872 | tf_op jit(solution)/shard_map/ppermute | solution.py:19
  16.2 14.7 %collective-permute-start.1 = (bf16[64,4096]{1,0:T(8,128)(2,1)}, bf16[64,4096]{1,0:T(8,128)(2,1)}, u32[]{:S(2)}, u32[]{:S(2)}) collective-permute-start(bf16[64,4096]{1,0:T(8,128)(2,1)} %param.10), channel_id=1, source_target_pairs={{0,32},{32,64},{64,96},{96,128},{128,160},{160,192},{192,224},{224... | collective-permute-start | bytes 1572872 | tf_op jit(solution)/shard_map/ppermute | solution.py:19
  16.2 4.5 %collective-permute-start.3 = (s32[256]{0:T(256)}, s32[256]{0:T(256)S(1)}, u32[]{:S(2)}, u32[]{:S(2)}) collective-permute-start(s32[256]{0:T(256)} %param.11), channel_id=1, source_target_pairs={{0,16},{16,0},{1,17},{17,1},{2,18},{18,2},{3,19},{19,3},{4,20},{20... | collective-permute-start | bytes 3080 | tf_op jit(solution)/shard_map/ppermute | solution.py:23
  16.6 4.2 %collective-permute-start.4 = (f32[256]{0:T(256)}, f32[256]{0:T(256)S(1)}, u32[]{:S(2)}, u32[]{:S(2)}) collective-permute-start(f32[256]{0:T(256)} %param.12), channel_id=1, source_target_pairs={{0,16},{16,0},{1,17},{17,1},{2,18},{18,2},{3,19},{19,3},{4,20},{20... | collective-permute-start | bytes 3080 | tf_op jit(solution)/shard_map/ppermute | solution.py:23
  20.7 25.8 %copy-start.11 = (bf16[64,4096]{1,0:T(8,128)(2,1)S(1)}, bf16[64,4096]{1,0:T(8,128)(2,1)}, u32[]{:S(2)}) copy-start(bf16[64,4096]{1,0:T(8,128)(2,1)} %param.10) | copy-start | bytes 1572868
  20.8 46.7 %copy-start.5 = (s32[512]{0:T(512)}, s32[512]{0:T(512)S(1)}, u32[]{:S(2)}) copy-start(s32[512]{0:T(512)S(1)} %pad_add_fusion) | copy-start | bytes 6148
  30.9 14.5 %copy-start.8 = (bf16[256,4096]{1,0:T(8,128)(2,1)}, bf16[256,4096]{1,0:T(8,128)(2,1)S(1)}, u32[]{:S(2)}) copy-start(bf16[256,4096]{1,0:T(8,128)(2,1)S(1)} %collective-permute-done.2.other_hbm) | copy-start | bytes 6291460
  30.9 12.5 %collective-permute-start.5 = (bf16[64,4096]{1,0:T(8,128)(2,1)}, bf16[64,4096]{1,0:T(8,128)(2,1)}, u32[]{:S(2)}, u32[]{:S(2)}) collective-permute-start(bf16[64,4096]{1,0:T(8,128)(2,1)} %collective-permute-done), channel_id=1, source_target_pairs={{0,224},{32,0},{64,32},{96,64},{128,96},{160,128},{192,160},{224,1... | collective-permute-start | bytes 1572872 | tf_op jit(solution)/shard_map/ppermute | solution.py:19
  31.3 13.7 %collective-permute-start.6 = (bf16[64,4096]{1,0:T(8,128)(2,1)}, bf16[64,4096]{1,0:T(8,128)(2,1)S(1)}, u32[]{:S(2)}, u32[]{:S(2)}) collective-permute-start(bf16[64,4096]{1,0:T(8,128)(2,1)} %collective-permute-done.1), channel_id=1, source_target_pairs={{0,32},{32,64},{64,96},{96,128},{128,160},{160,192},{192,224},{224... | collective-permute-start | bytes 1572872 | tf_op jit(solution)/shard_map/ppermute | solution.py:19
  33.1 34.4 %copy-start.1 = (s32[512,1]{1,0:T(8,128)}, s32[512,1]{1,0:T(8,128)S(1)}, u32[]{:S(2)}) copy-start(s32[512,1]{1,0:T(8,128)S(1)} %add.134.names_ref) | copy-start | bytes 6148
  35.5 12.6 %copy-start.7 = (bf16[512,4096]{1,0:T(8,128)(2,1)S(1)}, bf16[512,4096]{1,0:T(8,128)(2,1)}, u32[]{:S(2)}) copy-start(bf16[512,4096]{1,0:T(8,128)(2,1)} %constant_dynamic-update-slice_fusion) | copy-start | bytes 12582916
  45.0 11.7 %collective-permute-start.7 = (bf16[64,4096]{1,0:T(8,128)(2,1)}, bf16[64,4096]{1,0:T(8,128)(2,1)S(1)}, u32[]{:S(2)}, u32[]{:S(2)}) collective-permute-start(bf16[64,4096]{1,0:T(8,128)(2,1)} %collective-permute-done.5), channel_id=1, source_target_pairs={{0,224},{32,0},{64,32},{96,64},{128,96},{160,128},{192,160},{224,1... | collective-permute-start | bytes 1572872 | tf_op jit(solution)/shard_map/ppermute | solution.py:19
  45.4 13.3 %collective-permute-start.8 = (bf16[64,4096]{1,0:T(8,128)(2,1)S(1)}, bf16[64,4096]{1,0:T(8,128)(2,1)S(1)}, u32[]{:S(2)}, u32[]{:S(2)}) collective-permute-start(bf16[64,4096]{1,0:T(8,128)(2,1)S(1)} %collective-permute-done.6), channel_id=1, source_target_pairs={{0,32},{32,64},{64,96},{96,128},{128,160},{160,192},{192,224},{224... | collective-permute-start | bytes 1572872 | tf_op jit(solution)/shard_map/ppermute | solution.py:19
  48.1 1.3 copy-start.2
  56.7 5.7 %collective-permute-start.10 = (bf16[32,4096]{1,0:T(8,128)(2,1)S(1)}, bf16[32,4096]{1,0:T(8,128)(2,1)S(1)}, u32[]{:S(2)}, u32[]{:S(2)}) collective-permute-start(bf16[32,4096]{1,0:T(8,128)(2,1)S(1)} %slice.46), channel_id=1, source_target_pairs={{0,224},{32,0},{64,32},{96,64},{128,96},{160,128},{192,160},{224,1... | collective-permute-start | bytes 786440 | tf_op jit(solution)/shard_map/ppermute | solution.py:19
  58.9 7.1 %collective-permute-start.9 = (bf16[32,4096]{1,0:T(8,128)(2,1)S(1)}, bf16[32,4096]{1,0:T(8,128)(2,1)S(1)}, u32[]{:S(2)}, u32[]{:S(2)}) collective-permute-start(bf16[32,4096]{1,0:T(8,128)(2,1)S(1)} %slice.45), channel_id=1, source_target_pairs={{0,32},{32,64},{64,96},{96,128},{128,160},{160,192},{192,224},{224... | collective-permute-start | bytes 786440 | tf_op jit(solution)/shard_map/ppermute | solution.py:19
  67.5 21.2 %copy-start = (f32[512,512]{1,0:T(8,128)}, f32[512,512]{1,0:T(8,128)S(1)}, u32[]{:S(2)}) copy-start(f32[512,512]{1,0:T(8,128)S(1)} %pad_maximum_fusion.2.logits_ref) | copy-start | bytes 3145732
  67.9 0.7 copy-start.4
  68.6 20.1 %all-to-all-start = ((f32[32,3,512]{2,1,0:T(4,128)}), f32[32,3,512]{2,1,0:T(4,128)S(1)}, u32[]{:S(2)}, u32[]{:S(2)}) async-start(f32[32,3,512]{2,1,0:T(4,128)} %copy-done.4), calls=%async_computation | async-start | bytes 524288 | tf_op jit(solution)/shard_map/all_to_all | solution.py:250
  79.3 71.4 %reduce-scatter.2.cloned.1.call-start = ((), (), s32[]{:S(2)}) async-start(), calls=%async_computation.5 | async-start | bytes 4718592 | tf_op jit(solution)/shard_map/reduce_scatter | solution.py:298
  88.7 0.7 copy-start.9
  97.8 1.0 copy-start.6
  98.8 1.6 copy-start.3
  106.6 4.2 %collective-permute-start.11 = (bf16[4,256,1024]{2,1,0:T(8,128)(2,1)S(1)}, bf16[4,256,1024]{2,1,0:T(8,128)(2,1)S(1)}, u32[]{:S(2)}, u32[]{:S(2)}) collective-permute-start(bf16[4,256,1024]{2,1,0:T(8,128)(2,1)S(1)} %get-tuple-element.21), channel_id=1, source_target_pairs={{0,16},{16,0},{1,17},{17,1},{2,18},{18,2},{3,19},{19,3},{4,20},{20... | collective-permute-start | bytes 6291464 | tf_op jit(solution)/shard_map/ppermute | solution.py:23
  113.2 4.3 %copy-start.10 = (f32[32,3,512]{2,1,0:T(4,128)S(1)}, f32[32,3,512]{2,1,0:T(4,128)}, u32[]{:S(2)}) copy-start(f32[32,3,512]{2,1,0:T(4,128)} %copy-done.9) | copy-start | bytes 589828
  113.2 19.9 %all-to-all-start.1 = ((bf16[4,256,1024]{2,1,0:T(8,128)(2,1)}), bf16[4,256,1024]{2,1,0:T(8,128)(2,1)S(1)}, u32[]{:S(2)}, u32[]{:S(2)}) async-start(bf16[4,256,1024]{2,1,0:T(8,128)(2,1)} %add_convert_fusion), calls=%async_computation.1 | async-start | bytes 4194304 | tf_op jit(solution)/shard_map/all_to_all | solution.py:40
  134.4 10.6 %all-to-all-start.2 = ((bf16[4,256,256]{2,1,0:T(8,128)(2,1)}), bf16[4,256,256]{2,1,0:T(8,128)(2,1)S(1)}, u32[]{:S(2)}, u32[]{:S(2)}) async-start(bf16[4,256,256]{2,1,0:T(8,128)(2,1)} %pad_maximum_fusion.4), calls=%async_computation.2 | async-start | bytes 1048576 | tf_op jit(solution)/shard_map/all_to_all | solution.py:40
Sparse Core Ops, SparseCore 0:
  10.6 62.7 all-gather.1
  97.9 52.7 reduce-scatter.1
